TPU v7x, 128 devices: a whole 4x4x4 slice. The times are simulated.
128 devices in a mesh: grp: 2 (over z_hi), lon: 8 (over x, core), lat: 8 (over y, z_lo).
Axes of the slice: x: 4, y: 4, z: 4 (z_hi: 2, z_lo: 2; z = z_hi * 2 + z_lo), core: 2. Of those that a mesh axis runs over, the one named last changes fastest.
Arguments:
- tracer: float32 [2, 6, 8, 256, 1024], P('grp', None, None, 'lon', 'lat'), may hold values from -6 to 6
- velocity: float32 [2, 2, 8, 256, 1024], P('grp', None, None, 'lon', 'lat'), may hold values from -0.2 to 0.2
- mixing: float32 [2, 8], P('grp'), may hold values from 0.03 to 0.12
- vertical_mixing: float32 [2, 8], P('grp'), may hold values from 0.03 to 0.12
- transfer_coef: float32 [256, 1024], P('lon', 'lat'), may hold values from 0.05 to 0.5
- land_mask: int32 [256, 1024], P('lon', 'lat'), may hold values from 0 to 1, as said below
Outputs:
- advanced: float32 [2, 6, 8, 256, 1024], P('grp', None, None, 'lon', 'lat')
Inputs may be any that keep to these rules, and one draw needn't show every extreme that they name: `land_mask`: the share of ocean columns differs from block to block of 32 x 128 columns.
All inputs are finite; a program needn't handle non-finite values.
Results may differ from a plain program's by a relative error of at most 0.00002.
Values sent between devices are 32-bit elements; how exact they have to be, the bound alone decides.
A program may use at most 64 MiB of HBM per device.

v0:
```python
import jax
import jax.numpy as jnp
from jax import lax
from jax.sharding import PartitionSpec as P

SUBSTEPS = 4


OCEAN_SHARE = 0.5


def partner(block, axis, stride):
    count = lax.axis_size(axis)
    route = []
    for low in range(count):
        high = low | 1 << stride
        if high != low and high < count:
            route += [(low, high), (high, low)]
    return lax.ppermute(block, axis, route)


def padded_2(block, sides, width):
    for axis, dim in sides:
        count = lax.axis_size(axis)
        forward = [(i, i + 1) for i in range(count - 1)]
        backward = [(target, source) for source, target in forward]
        low = lax.ppermute(
            lax.slice_in_dim(block, block.shape[dim] - width, None, axis=dim), axis, forward
        )
        high = lax.ppermute(lax.slice_in_dim(block, 0, width, axis=dim), axis, backward)
        block = jnp.concatenate([low, block, high], axis=dim)
    return block


def advance(field, speeds, openness, horiz_mix, vert_mix):
    mix = horiz_mix[:, None, None]
    face_speed = 0.5 * (speeds[0, :, :-1, :] + speeds[0, :, 1:, :])
    face_open = openness[:-1, :] * openness[1:, :]
    west = field[..., :-1, :]
    east = field[..., 1:, :]
    flux_east = face_open * (face_speed * 0.5 * (west + east) - mix * (east - west))
    edge_row = jnp.zeros_like(flux_east[..., :1, :])
    padded_x = jnp.concatenate([edge_row, flux_east, edge_row], axis=-2)
    change_x = padded_x[..., :-1, :] - padded_x[..., 1:, :]
    side_speed = 0.5 * (speeds[1, :, :, :-1] + speeds[1, :, :, 1:])
    side_open = openness[:, :-1] * openness[:, 1:]
    south = field[..., :, :-1]
    north = field[..., :, 1:]
    flux_north = side_open * (side_speed * 0.5 * (south + north) - mix * (north - south))
    edge_col = jnp.zeros_like(flux_north[..., :, :1])
    padded_y = jnp.concatenate([edge_col, flux_north, edge_col], axis=-1)
    change_y = padded_y[..., :, :-1] - padded_y[..., :, 1:]
    lower = field[..., :-1, :, :]
    upper = field[..., 1:, :, :]
    flux_up = -vert_mix[:-1, None, None] * (upper - lower) * openness
    edge_level = jnp.zeros_like(flux_up[..., :1, :, :])
    padded_z = jnp.concatenate([edge_level, flux_up, edge_level], axis=-3)
    change_z = padded_z[..., :-1, :, :] - padded_z[..., 1:, :, :]
    return field + change_x + change_y + change_z


def split_coefficients(extended, levels):
    speeds_part = extended[: 2 * levels].reshape((2, levels) + extended.shape[1:])
    return (speeds_part, extended[2 * levels])


def body(tracer, velocity, mixing, vertical_mixing, transfer_coef, land_mask):
    is_ocean = lax.axis_index("grp") == 1
    fields = tracer[0]
    speeds = velocity[0]
    horiz_mix = mixing[0]
    vert_mix = vertical_mixing[0]
    levels = fields.shape[1]
    cells_x = fields.shape[2]
    cells_y = fields.shape[3]
    wet_cells = land_mask.astype(jnp.float32)
    surface = jnp.where(is_ocean, fields[:, 0], fields[:, levels - 1])
    remote = partner(surface, "grp", 0)
    ocean_top = jnp.where(is_ocean, surface, remote)
    atmosphere_bottom = jnp.where(is_ocean, remote, surface)
    surface_flux = transfer_coef * (ocean_top - atmosphere_bottom) * wet_cells
    fields = fields.at[:, levels - 1].add(jnp.where(is_ocean, 0.0, surface_flux))
    fields = fields.at[:, 0].add(jnp.where(is_ocean, -OCEAN_SHARE * surface_flux, 0.0))
    openness = jnp.where(is_ocean, wet_cells, jnp.ones_like(wet_cells))
    coefficients = jnp.concatenate(
        [speeds.reshape(2 * levels, cells_x, cells_y), openness[None]], axis=0
    )
    extended = padded_2(coefficients, (("lon", 1), ("lat", 2)), 1)
    speeds_ext, open_ext = split_coefficients(extended, levels)
    for substep in range(SUBSTEPS):
        padded = padded_2(fields, (("lon", 2), ("lat", 3)), 1)
        fields = advance(padded, speeds_ext, open_ext, horiz_mix, vert_mix)[:, :, 1:-1, 1:-1]
    return fields[None]


def solution(mesh):
    return jax.shard_map(
        body,
        mesh=mesh,
        in_specs=(
            P("grp", None, None, "lon", "lat"),
            P("grp", None, None, "lon", "lat"),
            P("grp", None),
            P("grp", None),
            P("lon", "lat"),
            P("lon", "lat"),
        ),
        out_specs=P("grp", None, None, "lon", "lat"),
        check_vma=False,
    )
```

profile of v0, /device:TPU:1, one launch (start us, length us, event | category | flops | bytes accessed | tf_op | source)
XLA Modules:
  0.0 124.6 jit_solution(9312843930533158963)
XLA Ops:
  1.7 4.5 %collective-permute-start.5 = (f32[17,1,128]{2,1,0:T(1,128)S(1)}, f32[17,1,128]{2,1,0:T(1,128)S(1)}, u32[]{:S(2)}, u32[]{:S(2)}) collective-permute-start(f32[17,1,128]{2,1,0:T(1,128)S(1)} %get-tuple-element.53), channel_id=1, source_target_pairs={{0,8},{8,16},{16,24},{24,32},{32,40},{40,48},{48,56},{1,9},{9,17},... | collective-permute-start | bytes 26120 | tf_op jit(solution)/shard_map/ppermute | solution.py:27
  6.2 1.9 %collective-permute-start.6 = (f32[17,1,128]{2,1,0:T(1,128)S(1)}, f32[17,1,128]{2,1,0:T(1,128)S(1)}, u32[]{:S(2)}, u32[]{:S(2)}) collective-permute-start(f32[17,1,128]{2,1,0:T(1,128)S(1)} %get-tuple-element.54), channel_id=1, source_target_pairs={{8,0},{16,8},{24,16},{32,24},{40,32},{48,40},{56,48},{9,1},{17,9},... | collective-permute-start | bytes 26120 | tf_op jit(solution)/shard_map/ppermute | solution.py:30
  8.1 1.2 copy.83
  9.3 3.7 %collective-permute-start = (f32[6,32,128]{2,1,0:T(8,128)S(1)}, f32[6,32,128]{2,1,0:T(8,128)S(1)}, u32[]{:S(2)}, u32[]{:S(2)}) collective-permute-start(f32[6,32,128]{2,1,0:T(8,128)S(1)} %fusion.15), channel_id=1, source_target_pairs={{0,64},{64,0},{1,65},{65,1},{2,66},{66,2},{3,67},{67,3},{4,68},{68... | collective-permute-start | bytes 294920 | tf_op jit(solution)/shard_map/ppermute | solution.py:19
  13.2 2.7 %collective-permute-start.7 = (f32[17,34,1]{2,1,0:T(8,128)S(1)}, f32[17,34,1]{2,1,0:T(8,128)S(1)}, u32[]{:S(2)}, u32[]{:S(2)}) collective-permute-start(f32[17,34,1]{2,1,0:T(8,128)S(1)} %get-tuple-element.51), channel_id=1, source_target_pairs={{0,1},{1,2},{2,3},{3,4},{4,5},{5,6},{6,7},{8,9},{9,10},{10,11},{11... | collective-permute-start | bytes 6944 | tf_op jit(solution)/shard_map/ppermute | solution.py:27
  15.9 1.3 %collective-permute-start.8 = (f32[17,34,1]{2,1,0:T(8,128)S(1)}, f32[17,34,1]{2,1,0:T(8,128)S(1)}, u32[]{:S(2)}, u32[]{:S(2)}) collective-permute-start(f32[17,34,1]{2,1,0:T(8,128)S(1)} %get-tuple-element.52), channel_id=1, source_target_pairs={{1,0},{2,1},{3,2},{4,3},{5,4},{6,5},{7,6},{9,8},{10,9},{11,10},{12... | collective-permute-start | bytes 6944 | tf_op jit(solution)/shard_map/ppermute | solution.py:30
  17.3 12.8 %collective-permute-done.7 = f32[17,34,1]{2,1,0:T(8,128)S(1)} collective-permute-done((f32[17,34,1]{2,1,0:T(8,128)S(1)}, f32[17,34,1]{2,1,0:T(8,128)S(1)}, u32[]{:S(2)}, u32[]{:S(2)}) %collective-permute-start.7) | collective-permute-done | bytes 2344 | tf_op jit(solution)/shard_map/ppermute | solution.py:27
  32.2 1.9 %scatter-add.9 = f32[6,8,32,128]{3,1,2,0:T(8,128)S(1)} dynamic-update-slice(f32[6,8,32,128]{3,1,2,0:T(8,128)S(1)} %copy.27, f32[6,1,32,128]{3,1,2,0:T(1,128)S(1)} %add.141, s32[]{:T(128)} %constant.73.clone.1, s32[]{:T(128)} %constant.73.clone.1, s32[]{:T(128)} %constant.73.clone.1, s32[]{:T(128)} %constant.73.clone.1) | dynamic-update-slice | bytes 196612 | tf_op jit(solution)/shard_map/scatter-add | solution.py:83
  34.2 4.6 %collective-permute-start.1 = (f32[6,8,1,128]{3,1,2,0:T(8,128)S(1)}, f32[6,8,1,128]{3,1,2,0:T(8,128)S(1)}, u32[]{:S(2)}, u32[]{:S(2)}) collective-permute-start(f32[6,8,1,128]{3,1,2,0:T(8,128)S(1)} %get-tuple-element.43), channel_id=1, source_target_pairs={{0,8},{8,16},{16,24},{24,32},{32,40},{40,48},{48,56},{1,9},{9,17},... | collective-permute-start | bytes 73736 | tf_op jit(solution)/shard_map/ppermute | solution.py:27
  38.8 1.9 %collective-permute-start.2 = (f32[6,8,1,128]{3,1,2,0:T(8,128)S(1)}, f32[6,8,1,128]{3,1,2,0:T(8,128)S(1)}, u32[]{:S(2)}, u32[]{:S(2)}) collective-permute-start(f32[6,8,1,128]{3,1,2,0:T(8,128)S(1)} %get-tuple-element.44), channel_id=1, source_target_pairs={{8,0},{16,8},{24,16},{32,24},{40,32},{48,40},{56,48},{9,1},{17,9},... | collective-permute-start | bytes 73736 | tf_op jit(solution)/shard_map/ppermute | solution.py:30
  40.8 3.1 %collective-permute-done.2 = f32[6,8,1,128]{3,1,2,0:T(8,128)S(1)} collective-permute-done((f32[6,8,1,128]{3,1,2,0:T(8,128)S(1)}, f32[6,8,1,128]{3,1,2,0:T(8,128)S(1)}, u32[]{:S(2)}, u32[]{:S(2)}) %collective-permute-start.2) | collective-permute-done | bytes 24608 | tf_op jit(solution)/shard_map/ppermute | solution.py:30
  45.1 1.3 %collective-permute-start.4 = (f32[6,8,34,1]{2,1,3,0:T(8,128)S(1)}, f32[6,8,34,1]{2,1,3,0:T(8,128)S(1)}, u32[]{:S(2)}, u32[]{:S(2)}) collective-permute-start(f32[6,8,34,1]{2,1,3,0:T(8,128)S(1)} %copy.58), channel_id=1, source_target_pairs={{1,0},{2,1},{3,2},{4,3},{5,4},{6,5},{7,6},{9,8},{10,9},{11,10},{12... | collective-permute-start | bytes 19592 | tf_op jit(solution)/shard_map/ppermute | solution.py:30
  46.4 4.7 %collective-permute-start.3 = (f32[6,8,34,1]{2,1,3,0:T(8,128)S(1)}, f32[6,8,34,1]{2,1,3,0:T(8,128)S(1)}, u32[]{:S(2)}, u32[]{:S(2)}) collective-permute-start(f32[6,8,34,1]{2,1,3,0:T(8,128)S(1)} %copy.57), channel_id=1, source_target_pairs={{0,1},{1,2},{2,3},{3,4},{4,5},{5,6},{6,7},{8,9},{9,10},{10,11},{11... | collective-permute-start | bytes 19592 | tf_op jit(solution)/shard_map/ppermute | solution.py:27
  56.6 2.8 %collective-permute-start.9 = (f32[6,8,1,128]{3,1,2,0:T(8,128)S(1)}, f32[6,8,1,128]{3,1,2,0:T(8,128)S(1)}, u32[]{:S(2)}, u32[]{:S(2)}) collective-permute-start(f32[6,8,1,128]{3,1,2,0:T(8,128)S(1)} %get-tuple-element.33), channel_id=1, source_target_pairs={{0,8},{8,16},{16,24},{24,32},{32,40},{40,48},{48,56},{1,9},{9,17},... | collective-permute-start | bytes 73736 | tf_op jit(solution)/shard_map/ppermute | solution.py:27
  59.4 1.9 %collective-permute-start.10 = (f32[6,8,1,128]{3,1,2,0:T(8,128)S(1)}, f32[6,8,1,128]{3,1,2,0:T(8,128)S(1)}, u32[]{:S(2)}, u32[]{:S(2)}) collective-permute-start(f32[6,8,1,128]{3,1,2,0:T(8,128)S(1)} %get-tuple-element.34), channel_id=1, source_target_pairs={{8,0},{16,8},{24,16},{32,24},{40,32},{48,40},{56,48},{9,1},{17,9},... | collective-permute-start | bytes 73736 | tf_op jit(solution)/shard_map/ppermute | solution.py:30
  61.6 2.9 %collective-permute-done.10 = f32[6,8,1,128]{3,1,2,0:T(8,128)S(1)} collective-permute-done((f32[6,8,1,128]{3,1,2,0:T(8,128)S(1)}, f32[6,8,1,128]{3,1,2,0:T(8,128)S(1)}, u32[]{:S(2)}, u32[]{:S(2)}) %collective-permute-start.10) | collective-permute-done | bytes 24608 | tf_op jit(solution)/shard_map/ppermute | solution.py:30
  65.3 4.5 %collective-permute-start.11 = (f32[6,8,34,1]{2,1,3,0:T(8,128)S(1)}, f32[6,8,34,1]{2,1,3,0:T(8,128)S(1)}, u32[]{:S(2)}, u32[]{:S(2)}) collective-permute-start(f32[6,8,34,1]{2,1,3,0:T(8,128)S(1)} %copy.63), channel_id=1, source_target_pairs={{0,1},{1,2},{2,3},{3,4},{4,5},{5,6},{6,7},{8,9},{9,10},{10,11},{11... | collective-permute-start | bytes 19592 | tf_op jit(solution)/shard_map/ppermute | solution.py:27
  70.3 1.5 %collective-permute-start.12 = (f32[6,8,34,1]{2,1,3,0:T(8,128)S(1)}, f32[6,8,34,1]{2,1,3,0:T(8,128)S(1)}, u32[]{:S(2)}, u32[]{:S(2)}) collective-permute-start(f32[6,8,34,1]{2,1,3,0:T(8,128)S(1)} %copy.64), channel_id=1, source_target_pairs={{1,0},{2,1},{3,2},{4,3},{5,4},{6,5},{7,6},{9,8},{10,9},{11,10},{12... | collective-permute-start | bytes 19592 | tf_op jit(solution)/shard_map/ppermute | solution.py:30
  72.3 4.1 %collective-permute-done.12 = f32[6,8,34,1]{2,1,3,0:T(8,128)S(1)} collective-permute-done((f32[6,8,34,1]{2,1,3,0:T(8,128)S(1)}, f32[6,8,34,1]{2,1,3,0:T(8,128)S(1)}, u32[]{:S(2)}, u32[]{:S(2)}) %collective-permute-start.12) | collective-permute-done | bytes 6560 | tf_op jit(solution)/shard_map/ppermute | solution.py:30
  80.0 3.1 %collective-permute-start.13 = (f32[6,8,1,128]{3,1,2,0:T(8,128)S(1)}, f32[6,8,1,128]{3,1,2,0:T(8,128)S(1)}, u32[]{:S(2)}, u32[]{:S(2)}) collective-permute-start(f32[6,8,1,128]{3,1,2,0:T(8,128)S(1)} %get-tuple-element.31), channel_id=1, source_target_pairs={{0,8},{8,16},{16,24},{24,32},{32,40},{40,48},{48,56},{1,9},{9,17},... | collective-permute-start | bytes 73736 | tf_op jit(solution)/shard_map/ppermute | solution.py:27
  83.1 1.9 %collective-permute-start.14 = (f32[6,8,1,128]{3,1,2,0:T(8,128)S(1)}, f32[6,8,1,128]{3,1,2,0:T(8,128)S(1)}, u32[]{:S(2)}, u32[]{:S(2)}) collective-permute-start(f32[6,8,1,128]{3,1,2,0:T(8,128)S(1)} %get-tuple-element.32), channel_id=1, source_target_pairs={{8,0},{16,8},{24,16},{32,24},{40,32},{48,40},{56,48},{9,1},{17,9},... | collective-permute-start | bytes 73736 | tf_op jit(solution)/shard_map/ppermute | solution.py:30
  85.3 2.9 %collective-permute-done.14 = f32[6,8,1,128]{3,1,2,0:T(8,128)S(1)} collective-permute-done((f32[6,8,1,128]{3,1,2,0:T(8,128)S(1)}, f32[6,8,1,128]{3,1,2,0:T(8,128)S(1)}, u32[]{:S(2)}, u32[]{:S(2)}) %collective-permute-start.14) | collective-permute-done | bytes 24608 | tf_op jit(solution)/shard_map/ppermute | solution.py:30
  89.1 4.7 %collective-permute-start.15 = (f32[6,8,34,1]{2,1,3,0:T(8,128)S(1)}, f32[6,8,34,1]{2,1,3,0:T(8,128)S(1)}, u32[]{:S(2)}, u32[]{:S(2)}) collective-permute-start(f32[6,8,34,1]{2,1,3,0:T(8,128)S(1)} %copy.65), channel_id=1, source_target_pairs={{0,1},{1,2},{2,3},{3,4},{4,5},{5,6},{6,7},{8,9},{9,10},{10,11},{11... | collective-permute-start | bytes 19592 | tf_op jit(solution)/shard_map/ppermute | solution.py:27
  94.3 1.3 %collective-permute-start.16 = (f32[6,8,34,1]{2,1,3,0:T(8,128)S(1)}, f32[6,8,34,1]{2,1,3,0:T(8,128)S(1)}, u32[]{:S(2)}, u32[]{:S(2)}) collective-permute-start(f32[6,8,34,1]{2,1,3,0:T(8,128)S(1)} %copy.66), channel_id=1, source_target_pairs={{1,0},{2,1},{3,2},{4,3},{5,4},{6,5},{7,6},{9,8},{10,9},{11,10},{12... | collective-permute-start | bytes 19592 | tf_op jit(solution)/shard_map/ppermute | solution.py:30
  96.0 2.8 %collective-permute-done.16 = f32[6,8,34,1]{2,1,3,0:T(8,128)S(1)} collective-permute-done((f32[6,8,34,1]{2,1,3,0:T(8,128)S(1)}, f32[6,8,34,1]{2,1,3,0:T(8,128)S(1)}, u32[]{:S(2)}, u32[]{:S(2)}) %collective-permute-start.16) | collective-permute-done | bytes 6560 | tf_op jit(solution)/shard_map/ppermute | solution.py:30
  102.5 3.4 %collective-permute-start.17 = (f32[6,8,1,128]{3,1,2,0:T(8,128)S(1)}, f32[6,8,1,128]{3,1,2,0:T(8,128)S(1)}, u32[]{:S(2)}, u32[]{:S(2)}) collective-permute-start(f32[6,8,1,128]{3,1,2,0:T(8,128)S(1)} %get-tuple-element.29), channel_id=1, source_target_pairs={{0,8},{8,16},{16,24},{24,32},{32,40},{40,48},{48,56},{1,9},{9,17},... | collective-permute-start | bytes 73736 | tf_op jit(solution)/shard_map/ppermute | solution.py:27
  106.0 1.9 %collective-permute-start.18 = (f32[6,8,1,128]{3,1,2,0:T(8,128)S(1)}, f32[6,8,1,128]{3,1,2,0:T(8,128)S(1)}, u32[]{:S(2)}, u32[]{:S(2)}) collective-permute-start(f32[6,8,1,128]{3,1,2,0:T(8,128)S(1)} %get-tuple-element.30), channel_id=1, source_target_pairs={{8,0},{16,8},{24,16},{32,24},{40,32},{48,40},{56,48},{9,1},{17,9},... | collective-permute-start | bytes 73736 | tf_op jit(solution)/shard_map/ppermute | solution.py:30
  108.2 2.9 %collective-permute-done.18 = f32[6,8,1,128]{3,1,2,0:T(8,128)S(1)} collective-permute-done((f32[6,8,1,128]{3,1,2,0:T(8,128)S(1)}, f32[6,8,1,128]{3,1,2,0:T(8,128)S(1)}, u32[]{:S(2)}, u32[]{:S(2)}) %collective-permute-start.18) | collective-permute-done | bytes 24608 | tf_op jit(solution)/shard_map/ppermute | solution.py:30
  111.9 2.9 %collective-permute-start.19 = (f32[6,8,34,1]{2,1,3,0:T(8,128)S(1)}, f32[6,8,34,1]{2,1,3,0:T(8,128)S(1)}, u32[]{:S(2)}, u32[]{:S(2)}) collective-permute-start(f32[6,8,34,1]{2,1,3,0:T(8,128)S(1)} %copy.67), channel_id=1, source_target_pairs={{0,1},{1,2},{2,3},{3,4},{4,5},{5,6},{6,7},{8,9},{9,10},{10,11},{11... | collective-permute-start | bytes 19592 | tf_op jit(solution)/shard_map/ppermute | solution.py:27
  115.3 1.5 %collective-permute-start.20 = (f32[6,8,34,1]{2,1,3,0:T(8,128)S(1)}, f32[6,8,34,1]{2,1,3,0:T(8,128)S(1)}, u32[]{:S(2)}, u32[]{:S(2)}) collective-permute-start(f32[6,8,34,1]{2,1,3,0:T(8,128)S(1)} %copy.68), channel_id=1, source_target_pairs={{1,0},{2,1},{3,2},{4,3},{5,4},{6,5},{7,6},{9,8},{10,9},{11,10},{12... | collective-permute-start | bytes 19592 | tf_op jit(solution)/shard_map/ppermute | solution.py:30
  117.3 2.6 %collective-permute-done.20 = f32[6,8,34,1]{2,1,3,0:T(8,128)S(1)} collective-permute-done((f32[6,8,34,1]{2,1,3,0:T(8,128)S(1)}, f32[6,8,34,1]{2,1,3,0:T(8,128)S(1)}, u32[]{:S(2)}, u32[]{:S(2)}) %collective-permute-start.20) | collective-permute-done | bytes 6560 | tf_op jit(solution)/shard_map/ppermute | solution.py:30
  122.3 1.3 %fusion.9 = f32[1,6,8,32,128]{4,2,3,1,0:T(8,128)S(1)} fusion(f32[6,7,34,130]{3,1,2,0:T(8,128)S(1)} %fusion.1, f32[6,8,34,129]{3,1,2,0:T(8,128)S(1)} %subtract_multiply_fusion, f32[6,8,34,130]{3,1,2,0:T(8,128)S(1)} %pad_maximum_fusion.6, f32[6,8,33,130]{3,1,2,0:T(8,128)S(1)} %subtract_multiply_fusion.4), kind=kLoop, calls=%fused_computation.41 | loop fusion | flops 1179648 | bytes 3981216 | tf_op jit(solution)/shard_map/broadcast_in_dim | solution.py:93
  (100 shorter events, 27.3 us)
Async XLA Ops:
  0.0 13.0 %copy-start = (f32[1,2,8,32,128]{4,3,2,1,0:T(8,128)S(1)}, f32[1,2,8,32,128]{4,3,2,1,0:T(8,128)}, u32[]{:S(2)}) copy-start(f32[1,2,8,32,128]{4,3,2,1,0:T(8,128)} %param.11) | copy-start | bytes 786436
  1.7 11.4 %collective-permute-start.5 = (f32[17,1,128]{2,1,0:T(1,128)S(1)}, f32[17,1,128]{2,1,0:T(1,128)S(1)}, u32[]{:S(2)}, u32[]{:S(2)}) collective-permute-start(f32[17,1,128]{2,1,0:T(1,128)S(1)} %get-tuple-element.53), channel_id=1, source_target_pairs={{0,8},{8,16},{16,24},{24,32},{32,40},{40,48},{48,56},{1,9},{9,17},... | collective-permute-start | bytes 26120 | tf_op jit(solution)/shard_map/ppermute | solution.py:27
  6.2 11.1 %copy-start.6 = (f32[1,8]{1,0:T(1,128)S(1)}, f32[1,8]{1,0:T(1,128)}, u32[]{:S(2)}) copy-start(f32[1,8]{1,0:T(1,128)} %param.13) | copy-start | bytes 100
  6.2 11.1 %copy-start.3 = (s32[32,128]{1,0:T(8,128)S(1)}, s32[32,128]{1,0:T(8,128)}, u32[]{:S(2)}) copy-start(s32[32,128]{1,0:T(8,128)} %param.15) | copy-start | bytes 49156
  6.2 6.8 %collective-permute-start.6 = (f32[17,1,128]{2,1,0:T(1,128)S(1)}, f32[17,1,128]{2,1,0:T(1,128)S(1)}, u32[]{:S(2)}, u32[]{:S(2)}) collective-permute-start(f32[17,1,128]{2,1,0:T(1,128)S(1)} %get-tuple-element.54), channel_id=1, source_target_pairs={{8,0},{16,8},{24,16},{32,24},{40,32},{48,40},{56,48},{9,1},{17,9},... | collective-permute-start | bytes 26120 | tf_op jit(solution)/shard_map/ppermute | solution.py:30
  9.3 22.0 %collective-permute-start = (f32[6,32,128]{2,1,0:T(8,128)S(1)}, f32[6,32,128]{2,1,0:T(8,128)S(1)}, u32[]{:S(2)}, u32[]{:S(2)}) collective-permute-start(f32[6,32,128]{2,1,0:T(8,128)S(1)} %fusion.15), channel_id=1, source_target_pairs={{0,64},{64,0},{1,65},{65,1},{2,66},{66,2},{3,67},{67,3},{4,68},{68... | collective-permute-start | bytes 294920 | tf_op jit(solution)/shard_map/ppermute | solution.py:19
  13.2 16.9 %collective-permute-start.7 = (f32[17,34,1]{2,1,0:T(8,128)S(1)}, f32[17,34,1]{2,1,0:T(8,128)S(1)}, u32[]{:S(2)}, u32[]{:S(2)}) collective-permute-start(f32[17,34,1]{2,1,0:T(8,128)S(1)} %get-tuple-element.51), channel_id=1, source_target_pairs={{0,1},{1,2},{2,3},{3,4},{4,5},{5,6},{6,7},{8,9},{9,10},{10,11},{11... | collective-permute-start | bytes 6944 | tf_op jit(solution)/shard_map/ppermute | solution.py:27
  15.9 14.2 %collective-permute-start.8 = (f32[17,34,1]{2,1,0:T(8,128)S(1)}, f32[17,34,1]{2,1,0:T(8,128)S(1)}, u32[]{:S(2)}, u32[]{:S(2)}) collective-permute-start(f32[17,34,1]{2,1,0:T(8,128)S(1)} %get-tuple-element.52), channel_id=1, source_target_pairs={{1,0},{2,1},{3,2},{4,3},{5,4},{6,5},{7,6},{9,8},{10,9},{11,10},{12... | collective-permute-start | bytes 6944 | tf_op jit(solution)/shard_map/ppermute | solution.py:30
  30.2 1.1 copy-start.1
  30.2 1.1 copy-start.2
  30.8 0.7 copy-start.4
  34.2 6.6 %collective-permute-start.1 = (f32[6,8,1,128]{3,1,2,0:T(8,128)S(1)}, f32[6,8,1,128]{3,1,2,0:T(8,128)S(1)}, u32[]{:S(2)}, u32[]{:S(2)}) collective-permute-start(f32[6,8,1,128]{3,1,2,0:T(8,128)S(1)} %get-tuple-element.43), channel_id=1, source_target_pairs={{0,8},{8,16},{16,24},{24,32},{32,40},{40,48},{48,56},{1,9},{9,17},... | collective-permute-start | bytes 73736 | tf_op jit(solution)/shard_map/ppermute | solution.py:27
  38.8 5.1 %collective-permute-start.2 = (f32[6,8,1,128]{3,1,2,0:T(8,128)S(1)}, f32[6,8,1,128]{3,1,2,0:T(8,128)S(1)}, u32[]{:S(2)}, u32[]{:S(2)}) collective-permute-start(f32[6,8,1,128]{3,1,2,0:T(8,128)S(1)} %get-tuple-element.44), channel_id=1, source_target_pairs={{8,0},{16,8},{24,16},{32,24},{40,32},{48,40},{56,48},{9,1},{17,9},... | collective-permute-start | bytes 73736 | tf_op jit(solution)/shard_map/ppermute | solution.py:30
  45.1 7.4 %collective-permute-start.4 = (f32[6,8,34,1]{2,1,3,0:T(8,128)S(1)}, f32[6,8,34,1]{2,1,3,0:T(8,128)S(1)}, u32[]{:S(2)}, u32[]{:S(2)}) collective-permute-start(f32[6,8,34,1]{2,1,3,0:T(8,128)S(1)} %copy.58), channel_id=1, source_target_pairs={{1,0},{2,1},{3,2},{4,3},{5,4},{6,5},{7,6},{9,8},{10,9},{11,10},{12... | collective-permute-start | bytes 19592 | tf_op jit(solution)/shard_map/ppermute | solution.py:30
  46.4 5.7 %collective-permute-start.3 = (f32[6,8,34,1]{2,1,3,0:T(8,128)S(1)}, f32[6,8,34,1]{2,1,3,0:T(8,128)S(1)}, u32[]{:S(2)}, u32[]{:S(2)}) collective-permute-start(f32[6,8,34,1]{2,1,3,0:T(8,128)S(1)} %copy.57), channel_id=1, source_target_pairs={{0,1},{1,2},{2,3},{3,4},{4,5},{5,6},{6,7},{8,9},{9,10},{10,11},{11... | collective-permute-start | bytes 19592 | tf_op jit(solution)/shard_map/ppermute | solution.py:27
  53.8 0.7 copy-start.5
  56.6 5.0 %collective-permute-start.9 = (f32[6,8,1,128]{3,1,2,0:T(8,128)S(1)}, f32[6,8,1,128]{3,1,2,0:T(8,128)S(1)}, u32[]{:S(2)}, u32[]{:S(2)}) collective-permute-start(f32[6,8,1,128]{3,1,2,0:T(8,128)S(1)} %get-tuple-element.33), channel_id=1, source_target_pairs={{0,8},{8,16},{16,24},{24,32},{32,40},{40,48},{48,56},{1,9},{9,17},... | collective-permute-start | bytes 73736 | tf_op jit(solution)/shard_map/ppermute | solution.py:27
  59.4 5.1 %collective-permute-start.10 = (f32[6,8,1,128]{3,1,2,0:T(8,128)S(1)}, f32[6,8,1,128]{3,1,2,0:T(8,128)S(1)}, u32[]{:S(2)}, u32[]{:S(2)}) collective-permute-start(f32[6,8,1,128]{3,1,2,0:T(8,128)S(1)} %get-tuple-element.34), channel_id=1, source_target_pairs={{8,0},{16,8},{24,16},{32,24},{40,32},{48,40},{56,48},{9,1},{17,9},... | collective-permute-start | bytes 73736 | tf_op jit(solution)/shard_map/ppermute | solution.py:30
  65.3 6.5 %collective-permute-start.11 = (f32[6,8,34,1]{2,1,3,0:T(8,128)S(1)}, f32[6,8,34,1]{2,1,3,0:T(8,128)S(1)}, u32[]{:S(2)}, u32[]{:S(2)}) collective-permute-start(f32[6,8,34,1]{2,1,3,0:T(8,128)S(1)} %copy.63), channel_id=1, source_target_pairs={{0,1},{1,2},{2,3},{3,4},{4,5},{5,6},{6,7},{8,9},{9,10},{10,11},{11... | collective-permute-start | bytes 19592 | tf_op jit(solution)/shard_map/ppermute | solution.py:27
  70.3 6.0 %collective-permute-start.12 = (f32[6,8,34,1]{2,1,3,0:T(8,128)S(1)}, f32[6,8,34,1]{2,1,3,0:T(8,128)S(1)}, u32[]{:S(2)}, u32[]{:S(2)}) collective-permute-start(f32[6,8,34,1]{2,1,3,0:T(8,128)S(1)} %copy.64), channel_id=1, source_target_pairs={{1,0},{2,1},{3,2},{4,3},{5,4},{6,5},{7,6},{9,8},{10,9},{11,10},{12... | collective-permute-start | bytes 19592 | tf_op jit(solution)/shard_map/ppermute | solution.py:30
  80.0 5.3 %collective-permute-start.13 = (f32[6,8,1,128]{3,1,2,0:T(8,128)S(1)}, f32[6,8,1,128]{3,1,2,0:T(8,128)S(1)}, u32[]{:S(2)}, u32[]{:S(2)}) collective-permute-start(f32[6,8,1,128]{3,1,2,0:T(8,128)S(1)} %get-tuple-element.31), channel_id=1, source_target_pairs={{0,8},{8,16},{16,24},{24,32},{32,40},{40,48},{48,56},{1,9},{9,17},... | collective-permute-start | bytes 73736 | tf_op jit(solution)/shard_map/ppermute | solution.py:27
  83.1 5.1 %collective-permute-start.14 = (f32[6,8,1,128]{3,1,2,0:T(8,128)S(1)}, f32[6,8,1,128]{3,1,2,0:T(8,128)S(1)}, u32[]{:S(2)}, u32[]{:S(2)}) collective-permute-start(f32[6,8,1,128]{3,1,2,0:T(8,128)S(1)} %get-tuple-element.32), channel_id=1, source_target_pairs={{8,0},{16,8},{24,16},{32,24},{40,32},{48,40},{56,48},{9,1},{17,9},... | collective-permute-start | bytes 73736 | tf_op jit(solution)/shard_map/ppermute | solution.py:30
  89.1 6.5 %collective-permute-start.15 = (f32[6,8,34,1]{2,1,3,0:T(8,128)S(1)}, f32[6,8,34,1]{2,1,3,0:T(8,128)S(1)}, u32[]{:S(2)}, u32[]{:S(2)}) collective-permute-start(f32[6,8,34,1]{2,1,3,0:T(8,128)S(1)} %copy.65), channel_id=1, source_target_pairs={{0,1},{1,2},{2,3},{3,4},{4,5},{5,6},{6,7},{8,9},{9,10},{10,11},{11... | collective-permute-start | bytes 19592 | tf_op jit(solution)/shard_map/ppermute | solution.py:27
  94.3 4.6 %collective-permute-start.16 = (f32[6,8,34,1]{2,1,3,0:T(8,128)S(1)}, f32[6,8,34,1]{2,1,3,0:T(8,128)S(1)}, u32[]{:S(2)}, u32[]{:S(2)}) collective-permute-start(f32[6,8,34,1]{2,1,3,0:T(8,128)S(1)} %copy.66), channel_id=1, source_target_pairs={{1,0},{2,1},{3,2},{4,3},{5,4},{6,5},{7,6},{9,8},{10,9},{11,10},{12... | collective-permute-start | bytes 19592 | tf_op jit(solution)/shard_map/ppermute | solution.py:30
  102.5 5.7 %collective-permute-start.17 = (f32[6,8,1,128]{3,1,2,0:T(8,128)S(1)}, f32[6,8,1,128]{3,1,2,0:T(8,128)S(1)}, u32[]{:S(2)}, u32[]{:S(2)}) collective-permute-start(f32[6,8,1,128]{3,1,2,0:T(8,128)S(1)} %get-tuple-element.29), channel_id=1, source_target_pairs={{0,8},{8,16},{16,24},{24,32},{32,40},{40,48},{48,56},{1,9},{9,17},... | collective-permute-start | bytes 73736 | tf_op jit(solution)/shard_map/ppermute | solution.py:27
  106.0 5.1 %collective-permute-start.18 = (f32[6,8,1,128]{3,1,2,0:T(8,128)S(1)}, f32[6,8,1,128]{3,1,2,0:T(8,128)S(1)}, u32[]{:S(2)}, u32[]{:S(2)}) collective-permute-start(f32[6,8,1,128]{3,1,2,0:T(8,128)S(1)} %get-tuple-element.30), channel_id=1, source_target_pairs={{8,0},{16,8},{24,16},{32,24},{40,32},{48,40},{56,48},{9,1},{17,9},... | collective-permute-start | bytes 73736 | tf_op jit(solution)/shard_map/ppermute | solution.py:30
  111.9 4.9 %collective-permute-start.19 = (f32[6,8,34,1]{2,1,3,0:T(8,128)S(1)}, f32[6,8,34,1]{2,1,3,0:T(8,128)S(1)}, u32[]{:S(2)}, u32[]{:S(2)}) collective-permute-start(f32[6,8,34,1]{2,1,3,0:T(8,128)S(1)} %copy.67), channel_id=1, source_target_pairs={{0,1},{1,2},{2,3},{3,4},{4,5},{5,6},{6,7},{8,9},{9,10},{10,11},{11... | collective-permute-start | bytes 19592 | tf_op jit(solution)/shard_map/ppermute | solution.py:27
  115.3 4.6 %collective-permute-start.20 = (f32[6,8,34,1]{2,1,3,0:T(8,128)S(1)}, f32[6,8,34,1]{2,1,3,0:T(8,128)S(1)}, u32[]{:S(2)}, u32[]{:S(2)}) collective-permute-start(f32[6,8,34,1]{2,1,3,0:T(8,128)S(1)} %copy.68), channel_id=1, source_target_pairs={{1,0},{2,1},{3,2},{4,3},{5,4},{6,5},{7,6},{9,8},{10,9},{11,10},{12... | collective-permute-start | bytes 19592 | tf_op jit(solution)/shard_map/ppermute | solution.py:30
where the time goes:
time: 125 us
  starting transfers between devices  58.1 us (46%)
  waiting for transfers between devices  34.3 us (27%)
  other arithmetic  16.5 us (13%)
  local copies, waits for them, and re-layouts  15.1 us (12%)
    ppermute x10, starting transfers between devices, padded_2(): lax.ppermute(lax.slice_in_dim(block, block.shape[dim] - width, None, axis...  37.9 us
    ppermute x10, waiting for transfers between devices, padded_2(): lax.ppermute(lax.slice_in_dim(block, 0, width, axis=dim), axis, backward)  21.4 us
    ppermute x10, starting transfers between devices, padded_2(): lax.ppermute(lax.slice_in_dim(block, 0, width, axis=dim), axis, backward)  16.4 us
    ppermute x10, waiting for transfers between devices, padded_2(): lax.ppermute(lax.slice_in_dim(block, block.shape[dim] - width, None, axis...  12.8 us
    unnamed x24, local copies, waits for them, and re-layouts  5.44 us
    ppermute x1, starting transfers between devices, partner(): return lax.ppermute(block, axis, route)  3.68 us
    concatenate x10, other arithmetic, padded_2(): block = jnp.concatenate([low, block, high], axis=dim)  3.54 us
    add x3, other arithmetic, advance(): return field + change_x + change_y + change_z  3.44 us
  transfers between devices with their start and end apart: 21, of which 8 were waited for; matrix products, arithmetic and copies ran while one was open for 6% of the time, Pallas kernels for 0%

commit v1 on v0

v1 whole, which is shorter than its diff:
```python
import jax
import jax.numpy as jnp
from jax import lax
from jax.experimental import pallas as pl
from jax.experimental.pallas import tpu as pltpu
from jax.sharding import PartitionSpec as P

SUBSTEPS = 4
OCEAN_SHARE = 0.5
T = 6
K = 8
CX, CY = 32, 128
R0, R1 = 12, 44
ROWS = 56
W = 4
SLOT = 20
MESH = pl.DeviceIdType.MESH


def kernel(tr, vel, mix, vmx, coef, mask, out, f0, f1, s0, s1, pw, pe, rw, re, uvs, cm, cs, res, msk, lsem, ssem, rsem):
    grp, lon, lat = lax.axis_index("grp"), lax.axis_index("lon"), lax.axis_index("lat")
    nlon, nlat = lax.axis_size("lon"), lax.axis_size("lat")
    ocean = grp == 1

    def level(k):
        return jnp.where(ocean, k, K - 1 - k)

    def exists(di, dj, sign=1):
        ok = None
        for pos, size, d in ((lon, nlon, di * sign), (lat, nlat, dj * sign)):
            if d:
                c = pos < size - 1 if d > 0 else pos > 0
                ok = c if ok is None else jnp.logical_and(ok, c)
        return ok

    def device(dg, di, dj):
        return {"grp": grp if dg == 0 else 1 - grp, "lon": lon + di, "lat": lat + dj}

    lo, hi, mid = slice(R0, R0 + W), slice(R1 - W, R1), slice(R0, R1)
    inlo, inhi = slice(R0 - W, R0), slice(R1, R1 + W)
    messages = []

    def message(where, src, dst):
        messages.append((where, src, dst))

    message((1, 0, 0), f0.at[0:T, 0, mid], f0.at[8, 2:8, mid])
    message((0, 1, 0), f0.at[0:8, :, hi], f0.at[0:8, :, inlo])
    message((0, -1, 0), f0.at[0:8, :, lo], f0.at[0:8, :, inhi])
    message((0, 1, 0), f0.at[8, 0:2, hi], f0.at[8, 0:2, inlo])
    message((0, -1, 0), f0.at[8, 0:2, lo], f0.at[8, 0:2, inhi])
    message((1, 1, 0), f0.at[0:T, 0, hi], f0.at[8, 2:8, inlo])
    message((1, -1, 0), f0.at[0:T, 0, lo], f0.at[8, 2:8, inhi])
    for dj, p, r in ((1, pw, rw), (-1, pe, re)):
        message((0, 0, dj), p.at[0:3, mid], r.at[0:3, mid])
        message((0, 1, dj), p.at[0:3, hi], r.at[0:3, inlo])
        message((0, -1, dj), p.at[0:3, lo], r.at[0:3, inhi])
        message((1, 0, dj), p.at[0, mid], r.at[3, mid])
        message((1, 1, dj), p.at[0, hi], r.at[3, inlo])
        message((1, -1, dj), p.at[0, lo], r.at[3, inhi])

    def remote(n):
        where, src, dst = messages[n]
        return pltpu.make_async_remote_copy(
            src_ref=src, dst_ref=dst, send_sem=ssem.at[n], recv_sem=rsem.at[n], device_id=device(*where), device_id_type=MESH
        )

    def guarded(ok, act):
        if ok is None:
            act()
        else:
            pl.when(ok)(act)

    loads = []
    for k in range(K):
        loads.append(pltpu.make_async_copy(tr.at[0, :, level(k)], f0.at[0:T, k, mid], lsem.at[k]))
        loads.append(pltpu.make_async_copy(vel.at[0, :, level(k)], f0.at[T : T + 2, k, mid], lsem.at[K + k]))
    loads.append(pltpu.make_async_copy(coef, f0.at[8, 1, mid], lsem.at[16]))
    loads.append(pltpu.make_async_copy(mask, msk, lsem.at[17]))

    def clear(ref, rows):
        shape = ref.shape[:-2] + (rows.stop - rows.start, CY)
        ref[..., rows, :] = jnp.zeros(shape, jnp.float32)

    @pl.when(lon == 0)
    def _():
        clear(f0, inlo), clear(rw, inlo), clear(re, inlo)

    @pl.when(lon == nlon - 1)
    def _():
        clear(f0, inhi), clear(rw, inhi), clear(re, inhi)

    @pl.when(lat == 0)
    def _():
        clear(rw, slice(R0 - W, R1 + W))

    @pl.when(lat == nlat - 1)
    def _():
        clear(re, slice(R0 - W, R1 + W))

    barrier = pltpu.get_barrier_semaphore()
    places = [(0, 0, 1), (0, 0, -1), (0, 1, 0), (0, -1, 0), (1, 0, 0)]
    places += [(0, a, b) for a in (1, -1) for b in (1, -1)]
    places += [(1, 1, 0), (1, -1, 0), (1, 0, 1), (1, 0, -1)]
    places += [(1, a, b) for a in (1, -1) for b in (1, -1)]
    met = 0
    for where in places:
        ok = exists(*where[1:])

        def greet(where=where):
            pl.semaphore_signal(barrier, inc=1, device_id=device(*where), device_id_type=MESH)

        guarded(ok, greet)
        met = met + (1 if ok is None else ok.astype(jnp.int32))

    for c in loads:
        c.start()
    for c in loads:
        c.wait()
    f0[8, 0, mid] = msk[...].astype(jnp.float32)

    lane = lax.broadcasted_iota(jnp.int32, (8, CY), 1)
    pos = lane % SLOT
    zero = jnp.zeros((8, CY), jnp.float32)

    def turn(x, shift):
        shift = shift % CY
        return x if shift == 0 else pltpu.roll(x, shift, 1)

    def between(a, b):
        return (lane >= a) & (lane < b)

    def pack(i, carry):
        rows = pl.ds(R0 + 8 * i, 8)
        for q in range(2):
            west, east = zero, zero
            for m in range(4):
                for t in range(T):
                    x = f0[t, 4 * q + m, rows]
                    at = t * SLOT + 4 * m
                    put = between(at, at + 4)
                    west = jnp.where(put, turn(x, at - (CY - W)), west)
                    east = jnp.where(put, turn(x, at), east)
            pw[q, rows], pe[q, rows] = west, east
        west, east = zero, zero
        for a in range(18):
            x = f0[6, a, rows] if a < 8 else f0[7, a - 8, rows] if a < 16 else f0[8, a - 16, rows]
            put = between(4 * a, 4 * a + 4)
            west = jnp.where(put, turn(x, 4 * a - (CY - W)), west)
            east = jnp.where(put, turn(x, 4 * a), east)
        pw[2, rows], pe[2, rows] = west, east
        return carry

    lax.fori_loop(0, 4, pack, 0)

    pl.semaphore_wait(barrier, met)
    for n, (where, _, _) in enumerate(messages):
        guarded(exists(*where[1:]), lambda n=n: remote(n).start())
    for n, (where, _, _) in enumerate(messages):
        guarded(exists(*where[1:], sign=-1), lambda n=n: remote(n).wait_recv())
        guarded(exists(*where[1:]), lambda n=n: remote(n).wait_send())

    def strips(i, carry):
        rows = pl.ds(pl.multiple_of(8 + 8 * i, 8), 8)
        far_w, far_e = pos < W, pos >= SLOT - W
        for k in range(K + 1):
            acc = zero
            for t in range(T):
                x = f0[t, k, rows] if k < K else f0[8, 2 + t, rows]
                at = t * SLOT
                acc = jnp.where(between(at + 4, at + 10), turn(x, at + 4), acc)
                acc = jnp.where(between(at + 10, at + 16), turn(x, at + 10 - 122), acc)
            q, m = (k // 4, k % 4) if k < K else (3, 0)
            acc = jnp.where(far_w, turn(rw[q, rows], -4 * m), acc)
            acc = jnp.where(far_e, turn(re[q, rows], 16 - 4 * m), acc)
            s0[k, rows] = jnp.where(lane < T * SLOT, acc, 0.0)
        for a in range(18):
            x = f0[6, a, rows] if a < 8 else f0[7, a - 8, rows] if a < 16 else f0[8, a - 16, rows]
            acc = jnp.where(between(4, 10), turn(x, 4), zero)
            acc = jnp.where(between(10, 16), turn(x, 10 - 122), acc)
            acc = jnp.where(between(0, 4), turn(rw[2, rows], -4 * a), acc)
            acc = jnp.where(between(16, 20), turn(re[2, rows], 16 - 4 * a), acc)
            two = acc + turn(acc, 20)
            uvs[a, rows] = two + turn(two, 40) + turn(two, 80)
        return carry

    lax.fori_loop(0, 5, strips, 0)

    sub = lax.broadcasted_iota(jnp.int32, (8, CY), 0)
    beyond_w = (pos < W) & (lat == 0)
    beyond_e = (pos >= SLOT - W) & (lat == nlat - 1)

    def opening(i, carry):
        rows = pl.ds(pl.multiple_of(8 + 8 * i, 8), 8)
        row = 8 + 8 * i + sub
        shut = ((row < R0) & (lon == 0)) | ((row >= R1) & (lon == nlon - 1))
        wet = f0[8, 0, rows]
        cm[6, 0, rows] = jnp.where(shut, 0.0, jnp.where(ocean, wet, 1.0))
        wet = uvs[16, rows]
        cs[6, 0, rows] = jnp.where(shut | beyond_w | beyond_e, 0.0, jnp.where(ocean, wet, 1.0))
        share = jnp.where(ocean, OCEAN_SHARE, 1.0)
        gain = share * f0[8, 1, rows] * f0[8, 0, rows]
        for t in range(T):
            x = f0[t, 0, rows]
            f0[t, 0, rows] = x + gain * (f0[8, 2 + t, rows] - x)
        x = s0[0, rows]
        s0[0, rows] = x + share * uvs[17, rows] * uvs[16, rows] * (s0[8, rows] - x)
        return carry

    lax.fori_loop(0, 5, opening, 0)

    def coefficients(c, u, v):
        def some_rows(i, carry):
            o = 8 + 8 * i
            rows = pl.ds(pl.multiple_of(o, 8), 8)
            before, after = pl.ds(o - 1, 8), pl.ds(o + 1, 8)
            w = c[6, 0, rows]
            wb, wa = w * c[6, 0, before], w * c[6, 0, after]
            ws, wn = w * turn(w, 1), w * turn(w, -1)
            below = None
            for k in range(K):
                h = mix[0, level(k)]
                uk, vk = u(k, rows), v(k, rows)
                sb, sa = 0.25 * (u(k, before) + uk), 0.25 * (u(k, after) + uk)
                ss, sn = 0.25 * (turn(vk, 1) + vk), 0.25 * (turn(vk, -1) + vk)
                c[1, k, rows] = wb * (sb + h)
                c[2, k, rows] = wa * (h - sa)
                c[3, k, rows] = ws * (ss + h)
                c[4, k, rows] = wn * (h - sn)
                own = 1.0 + (wb * (sb - h) - wa * (sa + h)) + (ws * (ss - h) - wn * (sn + h))
                if k > 0:
                    own = own - below
                if k < K - 1:
                    below = w * vmx[0, jnp.where(ocean, k, K - 2 - k)]
                    c[5, k, rows] = below
                    own = own - below
                c[0, k, rows] = own
            return carry

        lax.fori_loop(0, 5, some_rows, 0)

    coefficients(cm, lambda k, rows: f0[6, k, rows], lambda k, rows: f0[7, k, rows])
    coefficients(cs, lambda k, rows: uvs[k, rows], lambda k, rows: uvs[8 + k, rows])

    def substep(load, c, n, o, rows, store):
        before, after = pl.ds(o - 1, 8), pl.ds(o + 1, 8)
        own = [load(t, 0, rows) for t in range(n)]
        last = [None] * n
        below = None
        for k in range(K):
            co, cb, ca, cso, cno = (c[j, k, rows] for j in range(5))
            up = c[5, k, rows] if k < K - 1 else None
            for t in range(n):
                x = own[t]
                y = co * x + cb * load(t, k, before) + ca * load(t, k, after)
                y = y + cso * turn(x, 1) + cno * turn(x, -1)
                if k > 0:
                    y = y + below * last[t]
                if k < K - 1:
                    own[t] = load(t, k + 1, rows)
                    y = y + up * own[t]
                last[t] = x
                store(t, k, y)
            below = up

    def from_strip(k, rows, s):
        x = s[k, rows]
        return jnp.where((pos == 2) | (pos == 3), turn(x, -12), x)

    edge = (lane < 2) | (lane >= CY - 2)

    def advance(src, ssrc, dst, sdst, refresh):
        def some_rows(i, carry):
            o = 8 + 8 * i
            rows = pl.ds(pl.multiple_of(o, 8), 8)

            def keep(t, k, y):
                sdst[k, rows] = y

            substep(lambda t, k, r: ssrc[k, r], cs, 1, o, rows, keep)

            def put(t, k, y):
                if refresh:
                    if t == 0:
                        put.x = from_strip(k, rows, sdst)
                    y = jnp.where(edge, turn(put.x, 126 - (t * SLOT + 2)), y)
                dst[t, k, rows] = y

            substep(lambda t, k, r: src[t, k, r], cm, T, o, rows, put)
            return carry

        lax.fori_loop(0, 5, some_rows, 0)

    advance(f0, s0, f1, s1, False)
    advance(f1, s1, f0, s0, True)
    advance(f0, s0, f1, s1, False)

    def last_rows(i, carry):
        o = R0 + 8 * i
        rows = pl.ds(o, 8)

        def keep(t, k, y):
            s0[k, rows] = y

        substep(lambda t, k, r: s1[k, r], cs, 1, o, rows, keep)
        orows = pl.ds(pl.multiple_of(8 * i, 8), 8)

        def put(t, k, y):
            if t == 0:
                put.x = from_strip(k, rows, s0)
            res[t, k, orows] = jnp.where(edge, turn(put.x, 126 - (t * SLOT + 2)), y)

        substep(lambda t, k, r: f1[t, k, r], cm, T, o, rows, put)
        return carry

    lax.fori_loop(0, 4, last_rows, 0)

    stores = [pltpu.make_async_copy(res.at[:, k], out.at[0, :, level(k)], lsem.at[k]) for k in range(K)]
    for c in stores:
        c.start()
    for c in stores:
        c.wait()


N_MESSAGES = 19


def body(tracer, velocity, mixing, vertical_mixing, transfer_coef, land_mask):
    f32 = jnp.float32
    anywhere = pl.BlockSpec(memory_space=pl.ANY)
    scalars = pl.BlockSpec(memory_space=pltpu.SMEM)
    return pl.pallas_call(
        kernel,
        out_shape=jax.ShapeDtypeStruct(tracer.shape, f32),
        in_specs=[anywhere, anywhere, scalars, scalars, anywhere, anywhere],
        out_specs=anywhere,
        scratch_shapes=[
            pltpu.VMEM((9, K, ROWS, CY), f32),
            pltpu.VMEM((T, K, ROWS, CY), f32),
            pltpu.VMEM((K + 1, ROWS, CY), f32),
            pltpu.VMEM((K, ROWS, CY), f32),
            pltpu.VMEM((3, ROWS, CY), f32),
            pltpu.VMEM((3, ROWS, CY), f32),
            pltpu.VMEM((4, ROWS, CY), f32),
            pltpu.VMEM((4, ROWS, CY), f32),
            pltpu.VMEM((18, ROWS, CY), f32),
            pltpu.VMEM((7, K, ROWS, CY), f32),
            pltpu.VMEM((7, K, ROWS, CY), f32),
            pltpu.VMEM((T, K, CX, CY), f32),
            pltpu.VMEM((CX, CY), jnp.int32),
            pltpu.SemaphoreType.DMA((18,)),
            pltpu.SemaphoreType.DMA((N_MESSAGES,)),
            pltpu.SemaphoreType.DMA((N_MESSAGES,)),
        ],
        compiler_params=pltpu.CompilerParams(collective_id=0, has_side_effects=True),
        name="interval",
    )(tracer, velocity, mixing, vertical_mixing, transfer_coef, land_mask)


def solution(mesh):
    return jax.shard_map(
        body,
        mesh=mesh,
        in_specs=(
            P("grp", None, None, "lon", "lat"),
            P("grp", None, None, "lon", "lat"),
            P("grp", None),
            P("grp", None),
            P("lon", "lat"),
            P("lon", "lat"),
        ),
        out_specs=P("grp", None, None, "lon", "lat"),
        check_vma=False,
    )
```

time: 125 us -> 26.1 us (0.21)
  starting transfers between devices: 58.1 us -> 0 us
  waiting for transfers between devices: 34.3 us -> 0 us
  Pallas kernels: 0 us -> 23.8 us
  other arithmetic: 16.5 us -> 0 us
  local copies, waits for them, and re-layouts: 15.1 us -> 2.1 us
    ppermute x21 -> x0, starting transfers between devices: 58.1 us -> none  [the longest x10 37.9 us: padded_2(): lax.ppermute(lax.slice_in_dim(block, block.shape[dim] - width, None, axis...]
    ppermute x21 -> x0, waiting for transfers between devices: 34.3 us -> none  [the longest x10 21.4 us: padded_2(): lax.ppermute(lax.slice_in_dim(block, 0, width, axis=dim), axis, backward)]
    pallas_call x0 -> x1, Pallas kernels: none -> 23.8 us  [body(): pl.pallas_call(kernel, out_shape=jax.ShapeDtypeStruct(tracer.shape, f32),...]
    mul x16 -> x0, other arithmetic: 6.34 us -> none  [the longest x4 2.17 us: advance(): side_open * (side_speed * 0.5 * (south + north) - mix * (north - south))]
    ppermute x8 -> x0, local copies, waits for them, and re-layouts: 3.69 us -> none  [the longest x4 1.84 us: padded_2(): lax.ppermute(lax.slice_in_dim(block, block.shape[dim] - width, None, axis...]
    add x4 -> x0, other arithmetic: 3.54 us -> none  [the longest x3 3.44 us: advance(): return field + change_x + change_y + change_z]
    concatenate x10 -> x0, other arithmetic: 3.54 us -> none  [padded_2(): block = jnp.concatenate([low, block, high], axis=dim)]
    unnamed x24 -> x1, local copies, waits for them, and re-layouts: 5.44 us -> 2.1 us
  transfers between devices with their start and end apart: 21 -> 0, of which waited for: 8 -> 0; matrix products, arithmetic and copies ran while one was open for 6% -> 0% of each run, Pallas kernels for 0% -> 0%
where the time goes in v1:
time: 26.1 us; the launch traced here: 25.9 us
  Pallas kernels  23.8 us (91%)
  local copies, waits for them, and re-layouts  2.1 us (8%)
    pallas_call x1, Pallas kernels, body(): pl.pallas_call(kernel, out_shape=jax.ShapeDtypeStruct(tracer.shape, f32),...  23.8 us
    unnamed x1, local copies, waits for them, and re-layouts  2.1 us

profile of v1, /device:TPU:1, one launch (start us, length us, event | category | flops | bytes accessed | tf_op | source)
XLA Modules:
  0.0 25.9 jit_solution(10019109009174563101)
XLA Ops:
  0.0 23.8 %interval.1 = f32[1,6,8,32,128]{4,3,2,1,0:T(8,128)} custom-call(f32[1,6,8,32,128]{4,3,2,1,0:T(8,128)} %tr.1, f32[1,2,8,32,128]{4,3,2,1,0:T(8,128)} %vel.1, f32[1,8]{1,0:T(1,128)} %mix.1, f32[1,8]{1,0:T(1,128)} %vmx.1, f32[32,128]{1,0:T(8,128)} %coef.1, s32[32,128]{1,0:T(8,128)} %mask.1), custom_call_target="tpu_custom_call" | custom-call | tf_op jit(solution)/shard_map/interval/pallas_call | solution.py:331
  23.8 2.1 %copy.8 = f32[1,6,8,32,128]{4,3,2,1,0:T(8,128)} copy(f32[1,6,8,32,128]{4,3,2,1,0:T(8,128)} %interval.1) | data formatting | bytes 1572864

commit v2 on v0

v2 whole, which is shorter than its diff:
```python
import jax
import jax.numpy as jnp
from jax import lax
from jax.experimental import pallas as pl
from jax.experimental.pallas import tpu as pltpu
from jax.sharding import PartitionSpec as P

SUBSTEPS = 4
OCEAN_SHARE = 0.5
T = 6
K = 8
CX, CY = 32, 128
R0, R1 = 12, 44
ROWS = 56
W = 4
SLOT = 20
OWN = 8
SURFACE, U, V, WET, TRANSFER, PLANES = T, T + T * K, T + T * K + K, 70, 71, 72
FIELDS = 2 * K + 2
MESH = pl.DeviceIdType.MESH


def kernel(tr, vel, mix, vmx, coef, mask, out, f0, f1, sw0, sw1, se0, se1, pw, pe, rw, re, uw, ue, c, msk, lsem, ssem, rsem):
    grp, lon, lat = lax.axis_index("grp"), lax.axis_index("lon"), lax.axis_index("lat")
    nlon, nlat = lax.axis_size("lon"), lax.axis_size("lat")
    ocean = grp == 1

    def exists(di, dj, sign=1):
        ok = None
        for pos, size, d in ((lon, nlon, di * sign), (lat, nlat, dj * sign)):
            if d:
                one = pos < size - 1 if d > 0 else pos > 0
                ok = one if ok is None else jnp.logical_and(ok, one)
        return ok

    def device(dg, di, dj):
        return {"grp": grp if dg == 0 else 1 - grp, "lon": lon + di, "lat": lat + dj}

    def guarded(ok, act):
        if ok is None:
            act()
        else:
            pl.when(ok)(act)

    barrier = pltpu.get_barrier_semaphore()
    places = [(1, a, b) for a in (1, -1) for b in (1, -1)]
    places += [(0, a, b) for a in (1, -1) for b in (1, -1)]
    places += [(1, 1, 0), (1, -1, 0), (1, 0, 1), (1, 0, -1)]
    places += [(1, 0, 0), (0, 0, 1), (0, 0, -1), (0, 1, 0), (0, -1, 0)]
    for where in places:

        def greet(where=where):
            pl.semaphore_signal(barrier, inc=1, device_id=device(*where), device_id_type=MESH)

        guarded(exists(*where[1:]), greet)
    beside = (lon > 0).astype(jnp.int32) + (lon < nlon - 1).astype(jnp.int32)
    along = (lat > 0).astype(jnp.int32) + (lat < nlat - 1).astype(jnp.int32)
    met = 2 * (1 + beside) * (1 + along) - 1

    def level(k):
        return jnp.where(ocean, k, K - 1 - k)

    lo, hi, mid = pl.ds(R0, W), pl.ds(R1 - W, W), pl.ds(R0, CX)
    inlo, inhi = pl.ds(R0 - W, W), pl.ds(R1, W)

    def fetch(k, carry):
        pltpu.make_async_copy(tr.at[0, :, level(k)], f0.at[pl.ds(SURFACE + T * k, T), mid], lsem.at[0]).start()
        pltpu.make_async_copy(vel.at[0, 0, level(k)], f0.at[U + k, mid], lsem.at[0]).start()
        pltpu.make_async_copy(vel.at[0, 1, level(k)], f0.at[V + k, mid], lsem.at[0]).start()
        return carry

    pltpu.make_async_copy(mask, msk, lsem.at[1]).start()
    pltpu.make_async_copy(coef, f0.at[TRANSFER, mid], lsem.at[0]).start()
    lax.fori_loop(0, K, fetch, 0)

    def clear(ref, n, first, count):
        def one(j, carry):
            ref[j, pl.ds(first, count)] = jnp.zeros((count, CY), jnp.float32)
            return carry

        lax.fori_loop(0, n, one, 0)

    @pl.when(lon == 0)
    def _():
        clear(f0, PLANES, R0 - W, W), clear(rw, 4, R0 - W, W), clear(re, 4, R0 - W, W)

    @pl.when(lon == nlon - 1)
    def _():
        clear(f0, PLANES, R1, W), clear(rw, 4, R1, W), clear(re, 4, R1, W)

    @pl.when(lat == 0)
    def _():
        clear(rw, 4, R0 - W, CX + 2 * W)

    @pl.when(lat == nlat - 1)
    def _():
        clear(re, 4, R0 - W, CX + 2 * W)

    lane = lax.broadcasted_iota(jnp.int32, (8, CY), 1)
    sub = lax.broadcasted_iota(jnp.int32, (8, CY), 0)
    zero = jnp.zeros((8, CY), jnp.float32)
    pos = lane % SLOT
    ahead = (lane + W) % CY
    epos = ahead % SLOT
    far_w = (pos < W) & (lane < T * SLOT)
    far_e = (epos >= OWN) & (epos < OWN + W) & (ahead < T * SLOT)

    def turn(x, shift):
        shift = shift % CY
        return x if shift == 0 else pltpu.roll(x, shift, 1)

    def between(x, a, n):
        return (x >= a) & (x < a + n)

    pltpu.make_async_copy(mask, msk, lsem.at[1]).wait()
    total = pl.ds(0, T * K + 2 * K + 1)
    pltpu.make_async_copy(f0.at[total, mid], f0.at[total, mid], lsem.at[0]).wait()
    f0[WET, mid] = msk[...].astype(jnp.float32)

    def pack(i, carry):
        rows = pl.ds(R0 + 8 * i, 8)
        for q in range(2):
            west, east = zero, zero
            for m in range(4):
                for t in range(T):
                    x = f0[SURFACE + T * (4 * q + m) + t, rows]
                    at = t * SLOT + 4 * m
                    put = between(lane, at, W)
                    west = jnp.where(put, turn(x, at - (CY - W)), west)
                    east = jnp.where(put, turn(x, at), east)
            pw[q, rows], pe[q, rows] = west, east
        west, east = zero, zero
        for a in range(FIELDS):
            x = f0[U + a, rows]
            put = between(lane, 4 * a, W)
            west = jnp.where(put, turn(x, 4 * a - (CY - W)), west)
            east = jnp.where(put, turn(x, 4 * a), east)
        pw[2, rows], pe[2, rows] = west, east
        return carry

    lax.fori_loop(0, CX // 8, pack, 0)

    near, far = [], []
    for dj, p, r in ((1, pw, rw), (-1, pe, re)):
        packs = pl.ds(0, 3)
        near.append(((0, 0, dj), p.at[packs, mid], r.at[packs, mid]))
        near.append(((0, 1, dj), p.at[packs, hi], r.at[packs, inlo]))
        near.append(((0, -1, dj), p.at[packs, lo], r.at[packs, inhi]))
        far.append(((1, 0, dj), p.at[0, mid], r.at[3, mid]))
        far.append(((1, 1, dj), p.at[0, hi], r.at[3, inlo]))
        far.append(((1, -1, dj), p.at[0, lo], r.at[3, inhi]))
    block = pl.ds(SURFACE, PLANES - SURFACE)
    near.append(((0, 1, 0), f0.at[block, hi], f0.at[block, inlo]))
    near.append(((0, -1, 0), f0.at[block, lo], f0.at[block, inhi]))
    surface, other = pl.ds(SURFACE, T), pl.ds(0, T)
    far.append(((1, 1, 0), f0.at[surface, hi], f0.at[other, inlo]))
    far.append(((1, -1, 0), f0.at[surface, lo], f0.at[other, inhi]))
    far.append(((1, 0, 0), f0.at[surface, mid], f0.at[other, mid]))
    messages = near + far

    def remote(n):
        where, src, dst = messages[n]
        return pltpu.make_async_remote_copy(
            src_ref=src, dst_ref=dst, send_sem=ssem.at[n], recv_sem=rsem.at[n], device_id=device(*where), device_id_type=MESH
        )

    def arrived(n):
        guarded(exists(*messages[n][0][1:], sign=-1), lambda: remote(n).wait_recv())

    def sent(n):
        guarded(exists(*messages[n][0][1:]), lambda: remote(n).wait_send())

    pl.semaphore_wait(barrier, met)
    for n in range(len(messages)):
        guarded(exists(*messages[n][0][1:]), lambda n=n: remote(n).start())

    def pads(i, carry):
        rows = pl.ds(pl.multiple_of(8 + 8 * i, 8), 8)
        for t in range(T):
            f1[t, rows] = zero
            f1[T + T * K + t, rows] = zero
        for s in (sw0, se0, sw1, se1):
            s[0, rows] = zero
            s[K + 1, rows] = zero
        for j in range(3):
            c[j, 5, 0, rows] = zero
            c[j, 5, K, rows] = zero
        return carry

    lax.fori_loop(0, 5, pads, 0)

    def coefficients(side, o, rows, u, v):
        before, after = pl.ds(o - 1, 8), pl.ds(o + 1, 8)
        w = opening(side, o, rows)
        wb, wa = w * opening(side, o - 1, before), w * opening(side, o + 1, after)
        ws, wn = w * turn(w, 1), w * turn(w, -1)
        above = None
        for k in range(K):
            h = mix[0, level(k)]
            uk, vk = u(k, rows), v(k, rows)
            sb, sa = 0.25 * (u(k, before) + uk), 0.25 * (u(k, after) + uk)
            ss, sn = 0.25 * (turn(vk, 1) + vk), 0.25 * (turn(vk, -1) + vk)
            c[side, 1, k, rows] = wb * (sb + h)
            c[side, 2, k, rows] = wa * (h - sa)
            c[side, 3, k, rows] = ws * (ss + h)
            c[side, 4, k, rows] = wn * (h - sn)
            own = 1.0 + (wb * (sb - h) - wa * (sa + h)) + (ws * (ss - h) - wn * (sn + h))
            if k > 0:
                own = own - above
            if k < K - 1:
                above = w * vmx[0, jnp.where(ocean, k, K - 2 - k)]
                c[side, 5, k + 1, rows] = above
                own = own - above
            c[side, 0, k, rows] = own

    def opening(side, o, rows):
        row = o + sub
        shut = ((row < R0) & (lon == 0)) | ((row >= R1) & (lon == nlon - 1))
        if side == 1:
            shut = shut | (far_w & (lat == 0))
        if side == 2:
            shut = shut | (far_e & (lat == nlat - 1))
        wet = f0[WET, rows] if side == 0 else uw[2 * K, rows] if side == 1 else ue[2 * K, rows]
        return jnp.where(shut, 0.0, jnp.where(ocean, wet, 1.0))

    def own_strips(first, rows):
        west, east = zero, zero
        for t in range(T):
            x = f0[first + t, rows]
            at = t * SLOT
            west = jnp.where(between(lane, at + W, OWN), turn(x, at + W), west)
            east = jnp.where(between(ahead, at, OWN), turn(x, at - W - (CY - OWN)), east)
        return west, east

    def repeat(x):
        two = x + turn(x, SLOT)
        return two + turn(two, 2 * SLOT) + turn(two, 4 * SLOT)

    def inner(i, carry):
        @pl.when(i == 3)
        def _():
            for n in range(len(near)):
                arrived(n)

        o = pl.multiple_of(jnp.where(i < 3, 16 + 8 * i, 8 + 32 * (i - 3)), 8)
        rows = pl.ds(o, 8)
        for k in range(K):
            sw0[k + 1, rows], se0[k + 1, rows] = own_strips(SURFACE + T * k, rows)
        for a in range(FIELDS):
            x = f0[U + a, rows]
            uw[a, rows] = repeat(jnp.where(between(lane, W, OWN), turn(x, W), zero))
            ue[a, rows] = repeat(jnp.where(between(ahead, 0, OWN), turn(x, -W - (CY - OWN)), zero))
        coefficients(0, o, rows, lambda k, r: f0[U + k, r], lambda k, r: f0[V + k, r])
        return carry

    lax.fori_loop(0, 5, inner, 0)

    def outer(i, carry):
        rows = pl.ds(pl.multiple_of(8 + 8 * i, 8), 8)
        for k in range(K):
            q, m = k // 4, k % 4
            sw0[k + 1, rows] = jnp.where(far_w, turn(rw[q, rows], -4 * m), sw0[k + 1, rows])
            se0[k + 1, rows] = jnp.where(far_e, turn(re[q, rows], W - 4 * m), se0[k + 1, rows])
        for a in range(FIELDS):
            uw[a, rows] = uw[a, rows] + repeat(jnp.where(between(lane, 0, W), turn(rw[2, rows], -4 * a), zero))
            ue[a, rows] = ue[a, rows] + repeat(jnp.where(between(ahead, OWN, W), turn(re[2, rows], W - 4 * a), zero))
        return carry

    lax.fori_loop(0, 5, outer, 0)

    def edges(i, carry):
        o = 8 + 8 * i
        rows = pl.ds(pl.multiple_of(o, 8), 8)
        coefficients(1, o, rows, lambda k, r: uw[k, r], lambda k, r: uw[K + k, r])
        coefficients(2, o, rows, lambda k, r: ue[k, r], lambda k, r: ue[K + k, r])
        return carry

    lax.fori_loop(0, 5, edges, 0)
    for n in range(len(near)):
        sent(n)

    def stencil(side, src, n, k, o):
        rows, before, after = pl.ds(o, 8), pl.ds(o - 1, 8), pl.ds(o + 1, 8)
        co, cb, ca, cs, cn = (c[side, j, k, rows] for j in range(5))
        above, below = c[side, 5, k, rows], c[side, 5, k + 1, rows]
        for t in range(n):
            p = (k + 1) * n + t
            x = src[p, rows]
            y = co * x + cb * src[p, before] + ca * src[p, after]
            y = y + (cs * turn(x, 1) + cn * turn(x, -1))
            yield t, y + (above * src[p - n, rows] + below * src[p + n, rows])

    def substep(src, dst, first, last):
        def one(k, carry):
            for i in range(5):
                o = 8 + 8 * i
                for side, n in ((1, 1), (2, 1), (0, T)):
                    for t, y in stencil(side, src[side], n, k, o):
                        dst[side][(k + 1) * n + t, pl.ds(o, 8)] = y
            return carry

        lax.fori_loop(first, last, one, 0)

    def finish(src, first, last):
        stale = (lane < W) | (lane >= CY - W)

        def one(k, carry):
            for i in range(CX // 8):
                o = R0 + 8 * i
                ((_, west),) = stencil(1, src[1], 1, k, o)
                ((_, east),) = stencil(2, src[2], 1, k, o)
                fresh = jnp.where(pos < W, east, west)
                for t, y in stencil(0, src[0], T, k, o):
                    out[0, t, level(k), pl.ds(8 * i, 8)] = jnp.where(stale, turn(fresh, CY - W - t * SLOT), y)
            return carry

        lax.fori_loop(first, last, one, 0)

    share = jnp.where(ocean, OCEAN_SHARE, 1.0)

    def exchange(i, carry):
        rows = pl.ds(pl.multiple_of(8 + 8 * i, 8), 8)
        gain = share * f0[TRANSFER, rows] * f0[WET, rows]
        for t in range(T):
            x = f0[SURFACE + t, rows]
            f0[SURFACE + t, rows] = x + gain * (f0[t, rows] - x)
        west, east = own_strips(0, rows)
        west = jnp.where(far_w, rw[3, rows], west)
        east = jnp.where(far_e, turn(re[3, rows], W), east)
        for s, fields, theirs in ((sw0, uw, west), (se0, ue, east)):
            x = s[1, rows]
            s[1, rows] = x + share * fields[2 * K + 1, rows] * fields[2 * K, rows] * (theirs - x)
        return carry

    even, odd = (f0, sw0, se0), (f1, sw1, se1)

    def phase(late, carry):
        @pl.when(late == 1)
        def _():
            for n in range(len(near), len(messages)):
                sent(n)
            for n in range(len(near), len(messages)):
                arrived(n)
            lax.fori_loop(0, 5, exchange, 0)

        def bounds(s):
            return (s + 1) * (1 - late), K - late * (K - 1 - s)

        def two(j, carry):
            substep(even, odd, *bounds(1 + 2 * j))
            first, last = bounds(2 + 2 * j)
            substep(odd, even, first, first + (last - first) * (1 - j))
            finish(odd, first, first + (last - first) * j)
            return carry

        return lax.fori_loop(0, SUBSTEPS // 2, two, carry)

    lax.fori_loop(0, 2, phase, 0)


N_MESSAGES = 17


def body(tracer, velocity, mixing, vertical_mixing, transfer_coef, land_mask):
    f32 = jnp.float32
    anywhere = pl.BlockSpec(memory_space=pl.ANY)
    scalars = pl.BlockSpec(memory_space=pltpu.SMEM)

    def planes(*n):
        return pltpu.VMEM((*n, ROWS, CY), f32)

    return pl.pallas_call(
        kernel,
        out_shape=pltpu.VMEM(tracer.shape, f32),
        in_specs=[anywhere, anywhere, scalars, scalars, anywhere, anywhere],
        out_specs=pl.BlockSpec(memory_space=pltpu.VMEM),
        scratch_shapes=[
            planes(PLANES),
            planes(T * (K + 2)),
            *[planes(K + 2)] * 4,
            *[planes(3)] * 2,
            *[planes(4)] * 2,
            *[planes(FIELDS)] * 2,
            planes(3, 6, K + 1),
            pltpu.VMEM((CX, CY), jnp.int32),
            pltpu.SemaphoreType.DMA((2,)),
            pltpu.SemaphoreType.DMA((N_MESSAGES,)),
            pltpu.SemaphoreType.DMA((N_MESSAGES,)),
        ],
        compiler_params=pltpu.CompilerParams(collective_id=0, has_side_effects=True),
        name="interval",
    )(tracer, velocity, mixing, vertical_mixing, transfer_coef, land_mask)


def solution(mesh):
    return jax.shard_map(
        body,
        mesh=mesh,
        in_specs=(
            P("grp", None, None, "lon", "lat"),
            P("grp", None, None, "lon", "lat"),
            P("grp", None),
            P("grp", None),
            P("lon", "lat"),
            P("lon", "lat"),
        ),
        out_specs=P("grp", None, None, "lon", "lat"),
        check_vma=False,
    )
```

time: 125 us -> 21.1 us (0.17)
  the two profiles are of different devices: /device:TPU:1 before, /device:TPU:27 now
where the time goes in v2:
time: 21.1 us; the launch traced here: 20.9 us
  Pallas kernels  20 us (95%)
  local copies, waits for them, and re-layouts  0.88 us (4%)
    pallas_call x1, Pallas kernels, body(): pl.pallas_call(kernel, out_shape=pltpu.VMEM(tracer.shape, f32), in_specs=...  20 us
    unnamed x1, local copies, waits for them, and re-layouts  0.88 us

profile of v2, /device:TPU:27, one launch (start us, length us, event | category | flops | bytes accessed | tf_op | source)
XLA Modules:
  0.0 20.9 jit_solution(16072638093234583811)
XLA Ops:
  0.0 20.0 %interval.1 = f32[1,6,8,32,128]{4,3,2,1,0:T(8,128)S(1)} custom-call(f32[1,6,8,32,128]{4,3,2,1,0:T(8,128)} %tr.1, f32[1,2,8,32,128]{4,3,2,1,0:T(8,128)} %vel.1, f32[1,8]{1,0:T(1,128)} %mix.1, f32[1,8]{1,0:T(1,128)} %vmx.1, f32[32,128]{1,0:T(8,128)} %coef.1, s32[32,128]{1,0:T(8,128)} %mask.1), custom_call_target="tpu_custom_call" | custom-call | tf_op jit(solution)/shard_map/interval/pallas_call | solution.py:372
  20.0 0.9 %copy.8 = f32[1,6,8,32,128]{4,3,2,1,0:T(8,128)} copy(f32[1,6,8,32,128]{4,3,2,1,0:T(8,128)S(1)} %interval.1) | data formatting | bytes 1572864

commit v3 on v2

v3 whole, which is shorter than its diff:
```python
import jax
import jax.numpy as jnp
from jax import lax
from jax.experimental import pallas as pl
from jax.experimental.pallas import tpu as pltpu
from jax.sharding import PartitionSpec as P

SUBSTEPS = 4
OCEAN_SHARE = 0.5
T = 6
K = 8
CX, CY = 32, 128
R0, R1 = 12, 44
ROWS = 56
W = 4
SLOT = 16
OWN = 8
SURFACE, U, V, WET, TRANSFER, PLANES = T, T + T * K, T + T * K + K, 70, 71, 72
MESH = pl.DeviceIdType.MESH


def kernel(tr, vel, mix, vmx, coef, mask, out, f0, f1, f2, f3, sw0, sw1, se0, se1, pw, pe, rw, re, uw, ue, c, cw, ce, hs, msk, lsem, ssem, rsem):
    grp, lon, lat = lax.axis_index("grp"), lax.axis_index("lon"), lax.axis_index("lat")
    nlon, nlat = lax.axis_size("lon"), lax.axis_size("lat")
    ocean = grp == 1

    def exists(di, dj, sign=1):
        ok = None
        for pos, size, d in ((lon, nlon, di * sign), (lat, nlat, dj * sign)):
            if d:
                one = pos < size - 1 if d > 0 else pos > 0
                ok = one if ok is None else jnp.logical_and(ok, one)
        return ok

    def device(dg, di, dj):
        return {"grp": grp if dg == 0 else 1 - grp, "lon": lon + di, "lat": lat + dj}

    def guarded(ok, act):
        if ok is None:
            act()
        else:
            pl.when(ok)(act)

    barrier = pltpu.get_barrier_semaphore()
    places = [(1, a, b) for a in (1, -1) for b in (1, -1)]
    places += [(0, a, b) for a in (1, -1) for b in (1, -1)]
    places += [(1, 1, 0), (1, -1, 0), (1, 0, 1), (1, 0, -1)]
    places += [(1, 0, 0), (0, 0, 1), (0, 0, -1), (0, 1, 0), (0, -1, 0)]
    for where in places:

        def greet(where=where):
            pl.semaphore_signal(barrier, inc=1, device_id=device(*where), device_id_type=MESH)

        guarded(exists(*where[1:]), greet)
    beside = (lon > 0).astype(jnp.int32) + (lon < nlon - 1).astype(jnp.int32)
    along = (lat > 0).astype(jnp.int32) + (lat < nlat - 1).astype(jnp.int32)
    met = 2 * (1 + beside) * (1 + along) - 1

    def level(k):
        return jnp.where(ocean, k, K - 1 - k)

    lo, hi, mid = pl.ds(R0, W), pl.ds(R1 - W, W), pl.ds(R0, CX)
    inlo, inhi = pl.ds(R0 - W, W), pl.ds(R1, W)

    def fetch(k, carry):
        pltpu.make_async_copy(tr.at[0, :, level(k)], f0.at[pl.ds(SURFACE + T * k, T), mid], lsem.at[0]).start()
        pltpu.make_async_copy(vel.at[0, 0, level(k)], f0.at[U + k, mid], lsem.at[0]).start()
        pltpu.make_async_copy(vel.at[0, 1, level(k)], f0.at[V + k, mid], lsem.at[0]).start()
        return carry

    pltpu.make_async_copy(mask, msk, lsem.at[1]).start()
    pltpu.make_async_copy(coef, f0.at[TRANSFER, mid], lsem.at[0]).start()
    lax.fori_loop(0, K, fetch, 0)

    def clear(ref, n, first, count):
        def one(j, carry):
            ref[j, pl.ds(first, count)] = jnp.zeros((count, CY), jnp.float32)
            return carry

        lax.fori_loop(0, n, one, 0)

    @pl.when(lon == 0)
    def _():
        clear(f0, PLANES, R0 - W, W), clear(rw, 4, R0 - W, W), clear(re, 4, R0 - W, W)

    @pl.when(lon == nlon - 1)
    def _():
        clear(f0, PLANES, R1, W), clear(rw, 4, R1, W), clear(re, 4, R1, W)

    @pl.when(lat == 0)
    def _():
        clear(rw, 4, R0 - W, CX + 2 * W)

    @pl.when(lat == nlat - 1)
    def _():
        clear(re, 4, R0 - W, CX + 2 * W)

    lane = lax.broadcasted_iota(jnp.int32, (8, CY), 1)
    sub = lax.broadcasted_iota(jnp.int32, (8, CY), 0)
    zero = jnp.zeros((8, CY), jnp.float32)
    ahead = (lane + W) % CY
    slot = ahead // SLOT
    part = (lane % SLOT) // W
    far_w, far_e = part == 0, part == 1
    def turn(x, shift):
        shift = shift % CY
        return x if shift == 0 else pltpu.roll(x, shift, 1)

    def between(x, a, n):
        return (x >= a) & (x < a + n)

    pltpu.make_async_copy(mask, msk, lsem.at[1]).wait()
    total = pl.ds(0, T * K + 2 * K + 1)
    pltpu.make_async_copy(f0.at[total, mid], f0.at[total, mid], lsem.at[0]).wait()
    f0[WET, mid] = msk[...].astype(jnp.float32)

    def own_edges(ch, rows):
        acc = zero
        for k in range(K):
            x = f0[SURFACE + T * k + ch if ch < T else U + K * (ch - T) + k, rows]
            acc = jnp.where(slot == k, turn(x, SLOT * k + W), acc)
        return acc

    def pack(i, carry):
        rows = pl.ds(R0 + 8 * i, 8)
        west, east = [zero, zero, zero], [zero, zero, zero]
        for ch in range(T + 2):
            x, q, m = own_edges(ch, rows), ch // 4, ch % 4
            west[q] = jnp.where(part == m, turn(x, W * m), west[q])
            east[q] = jnp.where(part == m, turn(x, W * m - W), east[q])
            if ch < T:
                put = between(lane, W * (ch + 2), W)
                west[2] = jnp.where(put, turn(x, W * (ch + 2)), west[2])
                east[2] = jnp.where(put, turn(x, W * (ch + 1)), east[2])
        for j, plane in enumerate((WET, TRANSFER)):
            x, put = f0[plane, rows], between(lane, W * j, W)
            west[2] = jnp.where(put, turn(x, W * (j + 1)), west[2])
            east[2] = jnp.where(put, turn(x, W * j), east[2])
        for q in range(3):
            pw[q, rows], pe[q, rows] = west[q], east[q]
        return carry

    lax.fori_loop(0, CX // 8, pack, 0)

    near, far = [], []
    for dj, p, r in ((1, pw, rw), (-1, pe, re)):
        packs = pl.ds(0, 3)
        near.append(((0, 0, dj), p.at[packs, mid], r.at[packs, mid]))
        near.append(((0, 1, dj), p.at[packs, hi], r.at[packs, inlo]))
        near.append(((0, -1, dj), p.at[packs, lo], r.at[packs, inhi]))
        far.append(((1, 0, dj), p.at[2, mid], r.at[3, mid]))
        far.append(((1, 1, dj), p.at[2, hi], r.at[3, inlo]))
        far.append(((1, -1, dj), p.at[2, lo], r.at[3, inhi]))
    block = pl.ds(SURFACE, PLANES - SURFACE)
    near.append(((0, 1, 0), f0.at[block, hi], f0.at[block, inlo]))
    near.append(((0, -1, 0), f0.at[block, lo], f0.at[block, inhi]))
    surface, other = pl.ds(SURFACE, T), pl.ds(0, T)
    far.append(((1, 1, 0), f0.at[surface, hi], f0.at[other, inlo]))
    far.append(((1, -1, 0), f0.at[surface, lo], f0.at[other, inhi]))
    far.append(((1, 0, 0), f0.at[surface, mid], f0.at[other, mid]))
    messages = near + far

    def remote(n):
        where, src, dst = messages[n]
        return pltpu.make_async_remote_copy(
            src_ref=src, dst_ref=dst, send_sem=ssem.at[n], recv_sem=rsem.at[n], device_id=device(*where), device_id_type=MESH
        )

    def arrived(n):
        guarded(exists(*messages[n][0][1:], sign=-1), lambda: remote(n).wait_recv())

    def sent(n):
        guarded(exists(*messages[n][0][1:]), lambda: remote(n).wait_send())

    pl.semaphore_wait(barrier, met)
    for n in range(len(messages)):
        guarded(exists(*messages[n][0][1:]), lambda n=n: remote(n).start())

    def pads(i, carry):
        rows = pl.ds(pl.multiple_of(8 + 8 * i, 8), 8)
        for f in (f1, f2, f3):
            for t in range(T):
                f[t, rows] = zero
                f[T + T * K + t, rows] = zero
        c[5, 0, rows] = zero
        c[5, K, rows] = zero
        return carry

    lax.fori_loop(0, 5, pads, 0)

    def number(k):
        return vmx[0, jnp.where(ocean, k, K - 2 - k)]

    for side, its in enumerate((lane // SLOT, slot)):
        h, up, down = zero, zero, zero
        for k in range(K):
            h = jnp.where(its == k, mix[0, level(k)], h)
            if k > 0:
                up = jnp.where(its == k, number(k - 1), up)
            if k < K - 1:
                down = jnp.where(its == k, number(k), down)
        hs[side, 0], hs[side, 1], hs[side, 2] = h, up, down

    def faces(h, w, wb, wa, u, ub, ua, v):
        wb, wa = w * wb, w * wa
        ws, wn = w * turn(w, 1), w * turn(w, -1)
        sb, sa = 0.25 * (ub + u), 0.25 * (ua + u)
        ss, sn = 0.25 * (turn(v, 1) + v), 0.25 * (turn(v, -1) + v)
        own = 1.0 + (wb * (sb - h) - wa * (sa + h)) + (ws * (ss - h) - wn * (sn + h))
        return own, wb * (sb + h), wa * (h - sa), ws * (ss + h), wn * (h - sn)

    def opening(o, wet, beyond=False):
        row = o + sub
        shut = ((row < R0) & (lon == 0)) | ((row >= R1) & (lon == nlon - 1)) | beyond
        return jnp.where(shut, 0.0, jnp.where(ocean, wet, 1.0))

    def coefficients(o, rows):
        before, after = pl.ds(o - 1, 8), pl.ds(o + 1, 8)
        w, wb, wa = opening(o, f0[WET, rows]), opening(o - 1, f0[WET, before]), opening(o + 1, f0[WET, after])
        above = None
        for k in range(K):
            u, ub, ua = f0[U + k, rows], f0[U + k, before], f0[U + k, after]
            own, *others = faces(mix[0, level(k)], w, wb, wa, u, ub, ua, f0[V + k, rows])
            for j in range(4):
                c[1 + j, k, rows] = others[j]
            if k > 0:
                own = own - above
            if k < K - 1:
                above = w * number(k)
                c[5, k + 1, rows] = above
                own = own - above
            c[0, k, rows] = own

    def inner(i, carry):
        @pl.when(i == 3)
        def _():
            for n in range(len(near)):
                arrived(n)

        o = pl.multiple_of(jnp.where(i < 3, 16 + 8 * i, 8 + 32 * (i - 3)), 8)
        rows = pl.ds(o, 8)
        for ch in range(T + 2):
            x = own_edges(ch, rows)
            if ch < T:
                sw0[ch, rows], se0[ch, rows] = x, x
            else:
                uw[ch - T, rows], ue[ch - T, rows] = x, x
        coefficients(o, rows)
        return carry

    lax.fori_loop(0, 5, inner, 0)

    share = jnp.where(ocean, OCEAN_SHARE, 1.0)

    def repeat(x):
        x = x + turn(x, SLOT)
        x = x + turn(x, 2 * SLOT)
        return x + turn(x, 4 * SLOT)

    def outer(i, carry):
        o = 8 + 8 * i
        rows = pl.ds(pl.multiple_of(o, 8), 8)
        for ch in range(T + 2):
            q, m = ch // 4, ch % 4
            west, east = (sw0.at[ch], se0.at[ch]) if ch < T else (uw.at[ch - T], ue.at[ch - T])
            west[rows] = jnp.where(far_w, turn(rw[q, rows], -W * m), west[rows])
            east[rows] = jnp.where(far_e, turn(re[q, rows], W - W * m), east[rows])
        wet, transfer = turn(f0[WET, rows], W), turn(f0[TRANSFER, rows], W)
        first = slot == 0
        for r, fields, far, at, beyond in ((rw, uw, far_w & first, 0, lat == 0), (re, ue, far_e & first, W, lat == nlat - 1)):
            ours = between(lane, W, 2 * W) if r is rw else between(ahead, 0, 2 * W)
            near_wet = jnp.where(far, turn(r[2, rows], at), jnp.where(ours, wet, 0.0))
            gain = jnp.where(far, turn(r[2, rows], at - W), jnp.where(ours, transfer, 0.0))
            fields[2, rows] = opening(o, repeat(near_wet), (far_w if r is rw else far_e) & beyond)
            fields[3, rows] = share * gain * near_wet
        return carry

    lax.fori_loop(0, 5, outer, 0)

    def edges(i, carry):
        o = 8 + 8 * i
        rows, before, after = pl.ds(pl.multiple_of(o, 8), 8), pl.ds(o - 1, 8), pl.ds(o + 1, 8)
        for side, (fields, cs) in enumerate(((uw, cw), (ue, ce))):
            w = fields[2, rows]
            up, down = w * hs[side, 1], w * hs[side, 2]
            u = [fields[0, r] for r in (rows, before, after)]
            own, *others = faces(hs[side, 0], w, fields[2, before], fields[2, after], *u, fields[1, rows])
            for j, x in enumerate((own - up - down, *others, up, down)):
                cs[j, rows] = x
        return carry

    lax.fori_loop(0, 5, edges, 0)
    for n in range(len(near)):
        sent(n)

    def stencil(src, k, o):
        rows, before, after = pl.ds(o, 8), pl.ds(o - 1, 8), pl.ds(o + 1, 8)
        co, cb, ca, cs, cn = (c[j, k, rows] for j in range(5))
        up, down = c[5, k, rows], c[5, k + 1, rows]
        for t in range(T):
            p = SURFACE + T * k + t
            x = src[p, rows]
            y = co * x + cb * src[p, before] + ca * src[p, after]
            y = y + (cs * turn(x, 1) + cn * turn(x, -1))
            yield t, y + (up * src[p - T, rows] + down * src[p + T, rows])

    def substep(src, dst, first, pairs):
        def one(n, carry):
            for k in (first + 2 * n, first + 2 * n + 1):
                for i in range(5):
                    o = 8 + 8 * i
                    for t, y in stencil(src, k, o):
                        dst[SURFACE + T * k + t, pl.ds(o, 8)] = y
            return carry

        lax.fori_loop(0, pairs, one, 0)

    def strip_substep(west, east, wnext, enext):
        def some(half, carry):
            for i in range(5):
                o = 8 + 8 * i
                rows, before, after = pl.ds(o, 8), pl.ds(o - 1, 8), pl.ds(o + 1, 8)
                for src, dst, cs in ((west, wnext, cw), (east, enext, ce)):
                    co, cb, ca, cl, cr, up, down = (cs[j, rows] for j in range(7))
                    for t in range(T // 2):
                        t = half * (T // 2) + t
                        x = src[t, rows]
                        y = co * x + cb * src[t, before] + ca * src[t, after]
                        y = y + (cl * turn(x, 1) + cr * turn(x, -1))
                        dst[t, rows] = y + (up * turn(x, SLOT) + down * turn(x, -SLOT))
            return carry

        lax.fori_loop(0, 2, some, 0)

    def finish(n, carry):
        stale = (lane < W) | (lane >= CY - W)
        for k in (2 * n, 2 * n + 1):
            for i in range(CX // 8):
                o = R0 + 8 * i
                for t, y in stencil(f3, k, o):
                    fresh = jnp.where(far_w, se0[t, pl.ds(o, 8)], sw0[t, pl.ds(o, 8)])
                    fresh = pltpu.roll(fresh, CY - W - SLOT * k, 1)
                    out[0, t, level(k), pl.ds(8 * i, 8)] = jnp.where(stale, fresh, y)
        return carry

    def exchange(i, carry):
        rows = pl.ds(pl.multiple_of(8 + 8 * i, 8), 8)
        gain = share * f0[TRANSFER, rows] * f0[WET, rows]
        for t in range(T):
            x = f0[SURFACE + t, rows]
            f0[SURFACE + t, rows] = x + gain * (f0[t, rows] - x)
        for t in range(T):
            theirs = turn(f0[t, rows], W)
            west = jnp.where(far_w, turn(rw[3, rows], -W * (t + 2)), theirs)
            east = jnp.where(far_e, turn(re[3, rows], -W * (t + 1)), theirs)
            for s, fields, x in ((sw0, uw, west), (se0, ue, east)):
                s[t, rows] = s[t, rows] + fields[3, rows] * (x - s[t, rows])
        return carry

    def phase(late, carry):
        @pl.when(late == 1)
        def _():
            for n in range(len(near), len(messages)):
                sent(n)
            for n in range(len(near), len(messages)):
                arrived(n)
            lax.fori_loop(0, 5, exchange, 0)

        early = 1 - late
        substep(f0, f1, 2 * early, 1 + 2 * early)
        substep(f1, f2, 2 * early, 2 + early)
        substep(f2, f3, 4 * early, 2)
        return carry

    lax.fori_loop(0, 2, phase, 0)

    def strips(j, carry):
        strip_substep(sw0, se0, sw1, se1)
        strip_substep(sw1, se1, sw0, se0)
        return carry

    lax.fori_loop(0, SUBSTEPS // 2, strips, 0)
    lax.fori_loop(0, K // 2, finish, 0)


N_MESSAGES = 17


def body(tracer, velocity, mixing, vertical_mixing, transfer_coef, land_mask):
    f32 = jnp.float32
    anywhere = pl.BlockSpec(memory_space=pl.ANY)
    scalars = pl.BlockSpec(memory_space=pltpu.SMEM)

    def planes(*n):
        return pltpu.VMEM((*n, ROWS, CY), f32)

    return pl.pallas_call(
        kernel,
        out_shape=pltpu.VMEM(tracer.shape, f32),
        in_specs=[anywhere, anywhere, scalars, scalars, anywhere, anywhere],
        out_specs=pl.BlockSpec(memory_space=pltpu.VMEM),
        scratch_shapes=[
            planes(PLANES),
            *[planes(T * (K + 2))] * 3,
            *[planes(T)] * 4,
            *[planes(3)] * 2,
            *[planes(4)] * 4,
            planes(6, K + 1),
            *[planes(7)] * 2,
            pltpu.VMEM((2, 3, 8, CY), f32),
            pltpu.VMEM((CX, CY), jnp.int32),
            pltpu.SemaphoreType.DMA((2,)),
            pltpu.SemaphoreType.DMA((N_MESSAGES,)),
            pltpu.SemaphoreType.DMA((N_MESSAGES,)),
        ],
        compiler_params=pltpu.CompilerParams(collective_id=0, has_side_effects=True),
        name="interval",
    )(tracer, velocity, mixing, vertical_mixing, transfer_coef, land_mask)


def solution(mesh):
    return jax.shard_map(
        body,
        mesh=mesh,
        in_specs=(
            P("grp", None, None, "lon", "lat"),
            P("grp", None, None, "lon", "lat"),
            P("grp", None),
            P("grp", None),
            P("lon", "lat"),
            P("lon", "lat"),
        ),
        out_specs=P("grp", None, None, "lon", "lat"),
        check_vma=False,
    )
```

time: 21.1 us -> 19.8 us (0.938)
  Pallas kernels: 20 us -> 18.7 us
    pallas_call x1, Pallas kernels: 20 us -> 18.7 us  [body(): pl.pallas_call(kernel, out_shape=pltpu.VMEM(tracer.shape, f32), in_specs=...]
where the time goes in v3:
time: 19.8 us; the launch traced here: 19.6 us
  Pallas kernels  18.7 us (94%)
  local copies, waits for them, and re-layouts  0.88 us (4%)
    pallas_call x1, Pallas kernels, body(): pl.pallas_call(kernel, out_shape=pltpu.VMEM(tracer.shape, f32), in_specs=...  18.7 us
    unnamed x1, local copies, waits for them, and re-layouts  0.88 us

profile of v3, /device:TPU:27, one launch (start us, length us, event | category | flops | bytes accessed | tf_op | source)
XLA Modules:
  0.0 19.6 jit_solution(3404046364194201198)
XLA Ops:
  0.0 18.7 %interval.1 = f32[1,6,8,32,128]{4,3,2,1,0:T(8,128)S(1)} custom-call(f32[1,6,8,32,128]{4,3,2,1,0:T(8,128)} %tr.1, f32[1,2,8,32,128]{4,3,2,1,0:T(8,128)} %vel.1, f32[1,8]{1,0:T(1,128)} %mix.1, f32[1,8]{1,0:T(1,128)} %vmx.1, f32[32,128]{1,0:T(8,128)} %coef.1, s32[32,128]{1,0:T(8,128)} %mask.1), custom_call_target="tpu_custom_call" | custom-call | tf_op jit(solution)/shard_map/interval/pallas_call | solution.py:397
  18.7 0.9 %copy.8 = f32[1,6,8,32,128]{4,3,2,1,0:T(8,128)} copy(f32[1,6,8,32,128]{4,3,2,1,0:T(8,128)S(1)} %interval.1) | data formatting | bytes 1572864

commit v4 on v3

--- a/solution.py
+++ b/solution.py
@@ -173,7 +173,7 @@
         guarded(exists(*messages[n][0][1:]), lambda: remote(n).wait_send())
 
     pl.semaphore_wait(barrier, met)
-    for n in range(len(messages)):
+    for n in [0, 3, 1, 2, 4, 5, 6, 7, 16, 9, 10, 12, 13, 14, 15, 8, 11]:
         guarded(exists(*messages[n][0][1:]), lambda n=n: remote(n).start())
 
     def pads(i, carry):
@@ -316,21 +316,17 @@
         lax.fori_loop(0, pairs, one, 0)
 
     def strip_substep(west, east, wnext, enext):
-        def some(half, carry):
+        if True:
             for i in range(5):
                 o = 8 + 8 * i
                 rows, before, after = pl.ds(o, 8), pl.ds(o - 1, 8), pl.ds(o + 1, 8)
                 for src, dst, cs in ((west, wnext, cw), (east, enext, ce)):
                     co, cb, ca, cl, cr, up, down = (cs[j, rows] for j in range(7))
-                    for t in range(T // 2):
-                        t = half * (T // 2) + t
+                    for t in range(T):
                         x = src[t, rows]
                         y = co * x + cb * src[t, before] + ca * src[t, after]
                         y = y + (cl * turn(x, 1) + cr * turn(x, -1))
                         dst[t, rows] = y + (up * turn(x, SLOT) + down * turn(x, -SLOT))
-            return carry
-
-        lax.fori_loop(0, 2, some, 0)
 
     def finish(n, carry):
         stale = (lane < W) | (lane >= CY - W)

time: 19.8 us -> 19.3 us (0.975)
  Pallas kernels: 18.7 us -> 18.3 us
    pallas_call x1, Pallas kernels: 18.7 us -> 18.3 us  [body(): pl.pallas_call(kernel, out_shape=pltpu.VMEM(tracer.shape, f32), in_specs=...]
where the time goes in v4:
time: 19.3 us; the launch traced here: 19.1 us
  Pallas kernels  18.3 us (95%)
  local copies, waits for them, and re-layouts  0.88 us (5%)
    pallas_call x1, Pallas kernels, body(): pl.pallas_call(kernel, out_shape=pltpu.VMEM(tracer.shape, f32), in_specs=...  18.3 us
    unnamed x1, local copies, waits for them, and re-layouts  0.88 us

profile of v4, /device:TPU:27, one launch (start us, length us, event | category | flops | bytes accessed | tf_op | source)
XLA Modules:
  0.0 19.1 jit_solution(13635456515991197682)
XLA Ops:
  0.0 18.3 %interval.1 = f32[1,6,8,32,128]{4,3,2,1,0:T(8,128)S(1)} custom-call(f32[1,6,8,32,128]{4,3,2,1,0:T(8,128)} %tr.1, f32[1,2,8,32,128]{4,3,2,1,0:T(8,128)} %vel.1, f32[1,8]{1,0:T(1,128)} %mix.1, f32[1,8]{1,0:T(1,128)} %vmx.1, f32[32,128]{1,0:T(8,128)} %coef.1, s32[32,128]{1,0:T(8,128)} %mask.1), custom_call_target="tpu_custom_call" | custom-call | tf_op jit(solution)/shard_map/interval/pallas_call | solution.py:393
  18.3 0.9 %copy.8 = f32[1,6,8,32,128]{4,3,2,1,0:T(8,128)} copy(f32[1,6,8,32,128]{4,3,2,1,0:T(8,128)S(1)} %interval.1) | data formatting | bytes 1572864

commit v5 on v4

--- a/solution.py
+++ b/solution.py
@@ -173,7 +173,7 @@
         guarded(exists(*messages[n][0][1:]), lambda: remote(n).wait_send())
 
     pl.semaphore_wait(barrier, met)
-    for n in [0, 3, 1, 2, 4, 5, 6, 7, 16, 9, 10, 12, 13, 14, 15, 8, 11]:
+    for n in [0, 3, 1, 2, 4, 5, 9, 10, 12, 13, 6, 7, 16, 14, 15, 8, 11]:
         guarded(exists(*messages[n][0][1:]), lambda n=n: remote(n).start())
 
     def pads(i, carry):
@@ -235,6 +235,8 @@
         @pl.when(i == 3)
         def _():
             for n in range(len(near)):
+                sent(n)
+            for n in range(len(near)):
                 arrived(n)
 
         o = pl.multiple_of(jnp.where(i < 3, 16 + 8 * i, 8 + 32 * (i - 3)), 8)
@@ -290,8 +292,6 @@
         return carry
 
     lax.fori_loop(0, 5, edges, 0)
-    for n in range(len(near)):
-        sent(n)
 
     def stencil(src, k, o):
         rows, before, after = pl.ds(o, 8), pl.ds(o - 1, 8), pl.ds(o + 1, 8)
@@ -325,8 +325,15 @@
                     for t in range(T):
                         x = src[t, rows]
                         y = co * x + cb * src[t, before] + ca * src[t, after]
-                        y = y + (cl * turn(x, 1) + cr * turn(x, -1))
-                        dst[t, rows] = y + (up * turn(x, SLOT) + down * turn(x, -SLOT))
+                        dst[t, rows] = y + (cl * turn(x, 1) + cr * turn(x, -1))
+            for i in range(5):
+                o = 8 + 8 * i
+                rows, before, after = pl.ds(o, 8), pl.ds(o - 1, 8), pl.ds(o + 1, 8)
+                for src, dst, cs in ((west, wnext, cw), (east, enext, ce)):
+                    co, cb, ca, cl, cr, up, down = (cs[j, rows] for j in range(7))
+                    for t in range(T):
+                        x = src[t, rows]
+                        dst[t, rows] = dst[t, rows] + (up * turn(x, SLOT) + down * turn(x, -SLOT))
 
     def finish(n, carry):
         stale = (lane < W) | (lane >= CY - W)

time: 19.3 us -> 19.3 us (level)
  no operation moved by 1% of the time
where the time goes in v5:
time: 19.3 us; the launch traced here: 19.1 us
  Pallas kernels  18.3 us (95%)
  local copies, waits for them, and re-layouts  0.88 us (5%)
    pallas_call x1, Pallas kernels, body(): pl.pallas_call(kernel, out_shape=pltpu.VMEM(tracer.shape, f32), in_specs=...  18.3 us
    unnamed x1, local copies, waits for them, and re-layouts  0.88 us

profile of v5, /device:TPU:27, one launch (start us, length us, event | category | flops | bytes accessed | tf_op | source)
XLA Modules:
  0.0 19.1 jit_solution(5325676687571851886)
XLA Ops:
  0.0 18.3 %interval.1 = f32[1,6,8,32,128]{4,3,2,1,0:T(8,128)S(1)} custom-call(f32[1,6,8,32,128]{4,3,2,1,0:T(8,128)} %tr.1, f32[1,2,8,32,128]{4,3,2,1,0:T(8,128)} %vel.1, f32[1,8]{1,0:T(1,128)} %mix.1, f32[1,8]{1,0:T(1,128)} %vmx.1, f32[32,128]{1,0:T(8,128)} %coef.1, s32[32,128]{1,0:T(8,128)} %mask.1), custom_call_target="tpu_custom_call" | custom-call | tf_op jit(solution)/shard_map/interval/pallas_call | solution.py:400
  18.3 0.9 %copy.8 = f32[1,6,8,32,128]{4,3,2,1,0:T(8,128)} copy(f32[1,6,8,32,128]{4,3,2,1,0:T(8,128)S(1)} %interval.1) | data formatting | bytes 1572864

commit v6 on v5

--- a/solution.py
+++ b/solution.py
@@ -140,7 +140,7 @@
             pw[q, rows], pe[q, rows] = west[q], east[q]
         return carry
 
-    lax.fori_loop(0, CX // 8, pack, 0)
+    lax.fori_loop(0, CX // 8, pack, 0, unroll=2)
 
     near, far = [], []
     for dj, p, r in ((1, pw, rw), (-1, pe, re)):

time: 19.3 us -> 19.3 us (level)
  no operation moved by 1% of the time
where the time goes in v6:
time: 19.3 us; the launch traced here: 19.1 us
  Pallas kernels  18.3 us (95%)
  local copies, waits for them, and re-layouts  0.88 us (5%)
    pallas_call x1, Pallas kernels, body(): pl.pallas_call(kernel, out_shape=pltpu.VMEM(tracer.shape, f32), in_specs=...  18.3 us
    unnamed x1, local copies, waits for them, and re-layouts  0.88 us

profile of v6, /device:TPU:27, one launch (start us, length us, event | category | flops | bytes accessed | tf_op | source)
XLA Modules:
  0.0 19.1 jit_solution(7350813141058306697)
XLA Ops:
  0.0 18.3 %interval.1 = f32[1,6,8,32,128]{4,3,2,1,0:T(8,128)S(1)} custom-call(f32[1,6,8,32,128]{4,3,2,1,0:T(8,128)} %tr.1, f32[1,2,8,32,128]{4,3,2,1,0:T(8,128)} %vel.1, f32[1,8]{1,0:T(1,128)} %mix.1, f32[1,8]{1,0:T(1,128)} %vmx.1, f32[32,128]{1,0:T(8,128)} %coef.1, s32[32,128]{1,0:T(8,128)} %mask.1), custom_call_target="tpu_custom_call" | custom-call | tf_op jit(solution)/shard_map/interval/pallas_call | solution.py:400
  18.3 0.9 %copy.8 = f32[1,6,8,32,128]{4,3,2,1,0:T(8,128)} copy(f32[1,6,8,32,128]{4,3,2,1,0:T(8,128)S(1)} %interval.1) | data formatting | bytes 1572864
